TPU v7x, 256 devices: a whole 4x4x8 slice. The times are simulated.
256 devices in a mesh: tm: 8 (over x_hi, y), chan: 32 (over z, x_lo, core).
Axes of the slice: x: 4 (x_hi: 2, x_lo: 2; x = x_hi * 2 + x_lo), y: 4, z: 8, core: 2. Of those that a mesh axis runs over, the one named last changes fastest.
Arguments:
- vis: bfloat16 [512, 1024, 512], P('tm', 'chan'), may hold values from -6 to 6
- beam: bfloat16 [16, 1024, 2, 64, 256], P('tm', 'chan'), may hold values from -0.25 to 0.25
- fg_cov: float32 [1024, 1024], replicated, may hold values from 0 to 30, as said below
- flags: int32 [1024], replicated, may hold values 0 or 1
- m_modes: int32 [16], replicated, may hold values from 0 to 255, as said below
Outputs:
- filled: float32 [16, 2, 64, 1024], P('tm', None, None, 'chan')
Inputs may be any that keep to these rules, and one draw needn't show every extreme that they name: `m_modes`: m numbers of the window; entries may repeat. `fg_cov`: symmetric and positive definite.
All inputs are finite; a program needn't handle non-finite values.
Results may differ from a plain program's by a relative error of at most 0.0085.
Values sent between devices are 32-bit elements; how exact they have to be, the bound alone decides.
A program may use at most 64 MiB of HBM per device.

v0:
```python
import math

import jax
import jax.numpy as jnp
from jax import lax
from jax.sharding import PartitionSpec as P

ITERS = 10


EPS = 1e-06


def conjugate_fill(rows, good, apply_cov, curv_total, norm_total):

    def operator(vec):
        return vec + good * apply_cov(good * vec)

    start = good * rows
    norm_now = norm_total(start * start)[:, None]

    def advance(step, carry):
        sol, resid, direc, norm_now = carry
        image = operator(direc)
        alpha = norm_now / (curv_total(direc * image)[:, None] + EPS)
        sol = sol + alpha * direc
        resid = resid - alpha * image
        norm_next = norm_total(resid * resid)[:, None]
        direc = resid + norm_next / (norm_now + EPS) * direc
        return (sol, resid, direc, norm_next)

    sol, resid, direc, norm_now = lax.fori_loop(
        0, ITERS, advance, (jnp.zeros_like(rows), start, start, norm_now)
    )
    signal = apply_cov(good * sol)
    return good * rows + (1.0 - good) * signal


def per_device(vis, beam, fg_cov, flags, m_modes):
    t_dev = vis.shape[0]
    f_dev = vis.shape[1]
    width = vis.shape[2]
    half_width = width // 2
    n_time = t_dev * lax.axis_size("tm")
    m_dev = m_modes.shape[0] // lax.axis_size("tm")
    times = lax.axis_index("tm") * t_dev + jnp.arange(t_dev, dtype=jnp.int32)
    flat = vis.reshape(t_dev, f_dev * width)
    scale = 1.0 / math.sqrt(n_time)
    index = m_modes[:, None] * times[None, :] % n_time
    angle = 2.0 * math.pi / n_time * index.astype(jnp.float32)
    tables = jnp.concatenate([jnp.cos(angle), jnp.sin(angle)], axis=0).astype(jnp.bfloat16)
    prod = jnp.dot(tables, flat, preferred_element_type=jnp.float32).reshape(
        2, m_dev * lax.axis_size("tm"), f_dev, width
    )
    cos_part = prod[0]
    sin_part = prod[1]
    real_part = (cos_part[..., :half_width] + sin_part[..., half_width:]) * scale
    imag_part = (cos_part[..., half_width:] - sin_part[..., :half_width]) * scale
    mvis = lax.psum_scatter(
        jnp.concatenate([real_part, imag_part], axis=-1), "tm", scatter_dimension=0, tiled=True
    ).astype(jnp.bfloat16)
    prods = jnp.einsum(
        "mfpln,mfqn->mpqlf",
        beam,
        mvis.reshape(m_dev, f_dev, 2, half_width),
        preferred_element_type=jnp.float32,
    )
    coeffs = jnp.stack([prods[:, 0, 0] - prods[:, 1, 1], prods[:, 1, 0] + prods[:, 0, 1]], axis=1)
    degrees = coeffs.shape[2]
    good = (1 - flags).astype(jnp.float32)
    offset = lax.axis_index("chan") * f_dev
    good_here = lax.dynamic_slice_in_dim(good, offset, f_dev)
    cov_rows = lax.dynamic_slice_in_dim(fg_cov, offset, f_dev, 0)
    rows = coeffs.reshape(-1, f_dev)

    def spread_cov(vec):
        return lax.dot_general(
            lax.all_gather(vec, "chan", axis=1, tiled=True),
            cov_rows,
            (((1,), (1,)), ((), ())),
            precision=lax.Precision.HIGHEST,
            preferred_element_type=jnp.float32,
        )

    def curv_sum(values):
        return lax.psum(jnp.sum(values, axis=1), "chan")

    def norm_sum(values):
        return lax.psum(jnp.sum(values, axis=1), "chan")

    result = conjugate_fill(rows, good_here, spread_cov, curv_sum, norm_sum).reshape(
        m_dev, 2, degrees, f_dev
    )
    return result


def solution(mesh):
    placed = (P("tm", "chan", None), P("tm", "chan", None, None, None), P(), P(), P())
    return jax.shard_map(
        per_device,
        mesh=mesh,
        in_specs=placed,
        out_specs=P("tm", None, None, "chan"),
        check_vma=False,
    )
```

profile of v0, /device:TPU:1, one launch (start us, length us, event | category | flops | bytes accessed | tf_op | source)
XLA Modules:
  0.0 1975.6 jit_solution(2381233454197458835)
XLA Ops:
  6.5 2.8 copy.25
  10.1 0.6 copy.26
  10.7 0.6 copy.27
  11.5 1.1 pad_maximum_fusion
  12.8 0.9 constant_dynamic-slice_fusion
  13.7 78.5 %reduce-scatter.2.cloned.1.call-done = f32[2,32,512]{2,1,0:T(8,128)} async-done(((f32[16,32,512]{2,1,0:T(8,128)}), f32[2,32,512]{2,1,0:T(8,128)}) %reduce-scatter.2.cloned.1.call-update) | async-done | bytes 131088 | tf_op jit(solution)/shard_map/reduce_scatter | solution.py:59
  92.3 0.9 convert_element_type.12
  93.2 3.9 convolution_bitcast_fusion
  97.7 54.9 %psum.21 = f32[256,1]{0,1:T(1,128)S(1)} all-reduce(f32[256,1]{0,1:T(1,128)S(1)} %broadcast_in_dim.7), channel_id=1, replica_groups=mesh['tm'=8,'chan'=32] {'chan'}, use_global_device_ids=true, to_apply=%region_2.3 | all-reduce | flops 256 | bytes 2048 | tf_op jit(solution)/shard_map/psum | solution.py:89
  152.6 1748.1 %while.17 = (s32[]{:T(128)}, f32[256,32]{0,1:T(8,128)S(1)}, f32[256,32]{0,1:T(8,128)S(1)}, f32[256,32]{0,1:T(8,128)S(1)}, f32[256,1]{0,1:T(1,128)S(1)}, /*index=...) while((s32[]{:T(128)}, f32[256,32]{0,1:T(8,128)S(1)}, f32[256,32]{0,1:T(8,128)S(1)}, ...), condition=%wide.region_8.9_spmd.clone, body=%wide.region_3.8_spmd.clone.sunk | while | flops 100779008 | bytes 4836751 | solution.py:32
  152.6 0.7 broadcast_multiply_fusion.4
  153.4 64.9 %all-gather.5.cloned.1.call-done = f32[256,1024]{0,1:T(8,128)} async-done(((f32[256,32]{0,1:T(8,128)}), f32[256,1024]{0,1:T(8,128)}) %all-gather.5.cloned.1.call-update) | async-done | bytes 1048592 | tf_op jit(solution)/shard_map/while/body/eval_jaxpr/all_gather | solution.py:78
  218.3 1.9 multiply_reduce_fusion.5
  220.2 52.6 %psum.26 = f32[256]{0:T(256)S(1)} all-reduce(f32[256]{0:T(256)S(1)} %get-tuple-element.150), channel_id=1, replica_groups=mesh['tm'=8,'chan'=32] {'chan'}, use_global_device_ids=true, to_apply=%region_5.5 | all-reduce | flops 256 | bytes 2048 | tf_op jit(solution)/shard_map/while/body/eval_jaxpr/psum | solution.py:86
  272.9 54.6 %psum.27 = f32[256,1]{0,1:T(1,128)S(1)} all-reduce(f32[256,1]{0,1:T(1,128)S(1)} %bitcast.53), channel_id=1, replica_groups=mesh['tm'=8,'chan'=32] {'chan'}, use_global_device_ids=true, to_apply=%region_7.7 | all-reduce | flops 256 | bytes 2048 | tf_op jit(solution)/shard_map/while/body/eval_jaxpr/psum | solution.py:89
  327.6 0.7 broadcast_multiply_fusion.4
  328.3 64.9 %all-gather.5.cloned.1.call-done = f32[256,1024]{0,1:T(8,128)} async-done(((f32[256,32]{0,1:T(8,128)}), f32[256,1024]{0,1:T(8,128)}) %all-gather.5.cloned.1.call-update) | async-done | bytes 1048592 | tf_op jit(solution)/shard_map/while/body/eval_jaxpr/all_gather | solution.py:78
  393.2 1.9 multiply_reduce_fusion.5
  395.1 52.6 %psum.26 = f32[256]{0:T(256)S(1)} all-reduce(f32[256]{0:T(256)S(1)} %get-tuple-element.150), channel_id=1, replica_groups=mesh['tm'=8,'chan'=32] {'chan'}, use_global_device_ids=true, to_apply=%region_5.5 | all-reduce | flops 256 | bytes 2048 | tf_op jit(solution)/shard_map/while/body/eval_jaxpr/psum | solution.py:86
  447.8 54.6 %psum.27 = f32[256,1]{0,1:T(1,128)S(1)} all-reduce(f32[256,1]{0,1:T(1,128)S(1)} %bitcast.53), channel_id=1, replica_groups=mesh['tm'=8,'chan'=32] {'chan'}, use_global_device_ids=true, to_apply=%region_7.7 | all-reduce | flops 256 | bytes 2048 | tf_op jit(solution)/shard_map/while/body/eval_jaxpr/psum | solution.py:89
  502.5 0.7 broadcast_multiply_fusion.4
  503.2 64.6 %all-gather.5.cloned.1.call-done = f32[256,1024]{0,1:T(8,128)} async-done(((f32[256,32]{0,1:T(8,128)}), f32[256,1024]{0,1:T(8,128)}) %all-gather.5.cloned.1.call-update) | async-done | bytes 1048592 | tf_op jit(solution)/shard_map/while/body/eval_jaxpr/all_gather | solution.py:78
  567.9 1.9 multiply_reduce_fusion.5
  569.7 52.6 %psum.26 = f32[256]{0:T(256)S(1)} all-reduce(f32[256]{0:T(256)S(1)} %get-tuple-element.150), channel_id=1, replica_groups=mesh['tm'=8,'chan'=32] {'chan'}, use_global_device_ids=true, to_apply=%region_5.5 | all-reduce | flops 256 | bytes 2048 | tf_op jit(solution)/shard_map/while/body/eval_jaxpr/psum | solution.py:86
  622.4 54.6 %psum.27 = f32[256,1]{0,1:T(1,128)S(1)} all-reduce(f32[256,1]{0,1:T(1,128)S(1)} %bitcast.53), channel_id=1, replica_groups=mesh['tm'=8,'chan'=32] {'chan'}, use_global_device_ids=true, to_apply=%region_7.7 | all-reduce | flops 256 | bytes 2048 | tf_op jit(solution)/shard_map/while/body/eval_jaxpr/psum | solution.py:89
  677.1 0.7 broadcast_multiply_fusion.4
  677.9 64.6 %all-gather.5.cloned.1.call-done = f32[256,1024]{0,1:T(8,128)} async-done(((f32[256,32]{0,1:T(8,128)}), f32[256,1024]{0,1:T(8,128)}) %all-gather.5.cloned.1.call-update) | async-done | bytes 1048592 | tf_op jit(solution)/shard_map/while/body/eval_jaxpr/all_gather | solution.py:78
  742.5 1.9 multiply_reduce_fusion.5
  744.4 52.6 %psum.26 = f32[256]{0:T(256)S(1)} all-reduce(f32[256]{0:T(256)S(1)} %get-tuple-element.150), channel_id=1, replica_groups=mesh['tm'=8,'chan'=32] {'chan'}, use_global_device_ids=true, to_apply=%region_5.5 | all-reduce | flops 256 | bytes 2048 | tf_op jit(solution)/shard_map/while/body/eval_jaxpr/psum | solution.py:86
  797.1 54.6 %psum.27 = f32[256,1]{0,1:T(1,128)S(1)} all-reduce(f32[256,1]{0,1:T(1,128)S(1)} %bitcast.53), channel_id=1, replica_groups=mesh['tm'=8,'chan'=32] {'chan'}, use_global_device_ids=true, to_apply=%region_7.7 | all-reduce | flops 256 | bytes 2048 | tf_op jit(solution)/shard_map/while/body/eval_jaxpr/psum | solution.py:89
  851.8 0.7 broadcast_multiply_fusion.4
  852.5 64.6 %all-gather.5.cloned.1.call-done = f32[256,1024]{0,1:T(8,128)} async-done(((f32[256,32]{0,1:T(8,128)}), f32[256,1024]{0,1:T(8,128)}) %all-gather.5.cloned.1.call-update) | async-done | bytes 1048592 | tf_op jit(solution)/shard_map/while/body/eval_jaxpr/all_gather | solution.py:78
  917.1 1.9 multiply_reduce_fusion.5
  919.0 52.6 %psum.26 = f32[256]{0:T(256)S(1)} all-reduce(f32[256]{0:T(256)S(1)} %get-tuple-element.150), channel_id=1, replica_groups=mesh['tm'=8,'chan'=32] {'chan'}, use_global_device_ids=true, to_apply=%region_5.5 | all-reduce | flops 256 | bytes 2048 | tf_op jit(solution)/shard_map/while/body/eval_jaxpr/psum | solution.py:86
  971.7 54.6 %psum.27 = f32[256,1]{0,1:T(1,128)S(1)} all-reduce(f32[256,1]{0,1:T(1,128)S(1)} %bitcast.53), channel_id=1, replica_groups=mesh['tm'=8,'chan'=32] {'chan'}, use_global_device_ids=true, to_apply=%region_7.7 | all-reduce | flops 256 | bytes 2048 | tf_op jit(solution)/shard_map/while/body/eval_jaxpr/psum | solution.py:89
  1026.4 0.7 broadcast_multiply_fusion.4
  1027.1 65.0 %all-gather.5.cloned.1.call-done = f32[256,1024]{0,1:T(8,128)} async-done(((f32[256,32]{0,1:T(8,128)}), f32[256,1024]{0,1:T(8,128)}) %all-gather.5.cloned.1.call-update) | async-done | bytes 1048592 | tf_op jit(solution)/shard_map/while/body/eval_jaxpr/all_gather | solution.py:78
  1092.1 1.9 multiply_reduce_fusion.5
  1094.0 52.6 %psum.26 = f32[256]{0:T(256)S(1)} all-reduce(f32[256]{0:T(256)S(1)} %get-tuple-element.150), channel_id=1, replica_groups=mesh['tm'=8,'chan'=32] {'chan'}, use_global_device_ids=true, to_apply=%region_5.5 | all-reduce | flops 256 | bytes 2048 | tf_op jit(solution)/shard_map/while/body/eval_jaxpr/psum | solution.py:86
  1146.6 54.6 %psum.27 = f32[256,1]{0,1:T(1,128)S(1)} all-reduce(f32[256,1]{0,1:T(1,128)S(1)} %bitcast.53), channel_id=1, replica_groups=mesh['tm'=8,'chan'=32] {'chan'}, use_global_device_ids=true, to_apply=%region_7.7 | all-reduce | flops 256 | bytes 2048 | tf_op jit(solution)/shard_map/while/body/eval_jaxpr/psum | solution.py:89
  1201.3 0.7 broadcast_multiply_fusion.4
  1202.1 65.0 %all-gather.5.cloned.1.call-done = f32[256,1024]{0,1:T(8,128)} async-done(((f32[256,32]{0,1:T(8,128)}), f32[256,1024]{0,1:T(8,128)}) %all-gather.5.cloned.1.call-update) | async-done | bytes 1048592 | tf_op jit(solution)/shard_map/while/body/eval_jaxpr/all_gather | solution.py:78
  1267.0 1.9 multiply_reduce_fusion.5
  1268.9 52.6 %psum.26 = f32[256]{0:T(256)S(1)} all-reduce(f32[256]{0:T(256)S(1)} %get-tuple-element.150), channel_id=1, replica_groups=mesh['tm'=8,'chan'=32] {'chan'}, use_global_device_ids=true, to_apply=%region_5.5 | all-reduce | flops 256 | bytes 2048 | tf_op jit(solution)/shard_map/while/body/eval_jaxpr/psum | solution.py:86
  1321.6 54.6 %psum.27 = f32[256,1]{0,1:T(1,128)S(1)} all-reduce(f32[256,1]{0,1:T(1,128)S(1)} %bitcast.53), channel_id=1, replica_groups=mesh['tm'=8,'chan'=32] {'chan'}, use_global_device_ids=true, to_apply=%region_7.7 | all-reduce | flops 256 | bytes 2048 | tf_op jit(solution)/shard_map/while/body/eval_jaxpr/psum | solution.py:89
  1376.3 0.7 broadcast_multiply_fusion.4
  1377.0 64.9 %all-gather.5.cloned.1.call-done = f32[256,1024]{0,1:T(8,128)} async-done(((f32[256,32]{0,1:T(8,128)}), f32[256,1024]{0,1:T(8,128)}) %all-gather.5.cloned.1.call-update) | async-done | bytes 1048592 | tf_op jit(solution)/shard_map/while/body/eval_jaxpr/all_gather | solution.py:78
  1442.0 1.9 multiply_reduce_fusion.5
  1443.9 52.6 %psum.26 = f32[256]{0:T(256)S(1)} all-reduce(f32[256]{0:T(256)S(1)} %get-tuple-element.150), channel_id=1, replica_groups=mesh['tm'=8,'chan'=32] {'chan'}, use_global_device_ids=true, to_apply=%region_5.5 | all-reduce | flops 256 | bytes 2048 | tf_op jit(solution)/shard_map/while/body/eval_jaxpr/psum | solution.py:86
  1496.5 54.6 %psum.27 = f32[256,1]{0,1:T(1,128)S(1)} all-reduce(f32[256,1]{0,1:T(1,128)S(1)} %bitcast.53), channel_id=1, replica_groups=mesh['tm'=8,'chan'=32] {'chan'}, use_global_device_ids=true, to_apply=%region_7.7 | all-reduce | flops 256 | bytes 2048 | tf_op jit(solution)/shard_map/while/body/eval_jaxpr/psum | solution.py:89
  1551.2 0.7 broadcast_multiply_fusion.4
  1552.0 64.6 %all-gather.5.cloned.1.call-done = f32[256,1024]{0,1:T(8,128)} async-done(((f32[256,32]{0,1:T(8,128)}), f32[256,1024]{0,1:T(8,128)}) %all-gather.5.cloned.1.call-update) | async-done | bytes 1048592 | tf_op jit(solution)/shard_map/while/body/eval_jaxpr/all_gather | solution.py:78
  1616.6 1.9 multiply_reduce_fusion.5
  1618.5 52.6 %psum.26 = f32[256]{0:T(256)S(1)} all-reduce(f32[256]{0:T(256)S(1)} %get-tuple-element.150), channel_id=1, replica_groups=mesh['tm'=8,'chan'=32] {'chan'}, use_global_device_ids=true, to_apply=%region_5.5 | all-reduce | flops 256 | bytes 2048 | tf_op jit(solution)/shard_map/while/body/eval_jaxpr/psum | solution.py:86
  1671.2 54.6 %psum.27 = f32[256,1]{0,1:T(1,128)S(1)} all-reduce(f32[256,1]{0,1:T(1,128)S(1)} %bitcast.53), channel_id=1, replica_groups=mesh['tm'=8,'chan'=32] {'chan'}, use_global_device_ids=true, to_apply=%region_7.7 | all-reduce | flops 256 | bytes 2048 | tf_op jit(solution)/shard_map/while/body/eval_jaxpr/psum | solution.py:89
  1725.9 0.7 broadcast_multiply_fusion.4
  1726.6 64.9 %all-gather.5.cloned.1.call-done = f32[256,1024]{0,1:T(8,128)} async-done(((f32[256,32]{0,1:T(8,128)}), f32[256,1024]{0,1:T(8,128)}) %all-gather.5.cloned.1.call-update) | async-done | bytes 1048592 | tf_op jit(solution)/shard_map/while/body/eval_jaxpr/all_gather | solution.py:78
  1791.5 1.9 multiply_reduce_fusion.5
  1793.4 52.6 %psum.26 = f32[256]{0:T(256)S(1)} all-reduce(f32[256]{0:T(256)S(1)} %get-tuple-element.150), channel_id=1, replica_groups=mesh['tm'=8,'chan'=32] {'chan'}, use_global_device_ids=true, to_apply=%region_5.5 | all-reduce | flops 256 | bytes 2048 | tf_op jit(solution)/shard_map/while/body/eval_jaxpr/psum | solution.py:86
  1846.1 54.6 %psum.27 = f32[256,1]{0,1:T(1,128)S(1)} all-reduce(f32[256,1]{0,1:T(1,128)S(1)} %bitcast.53), channel_id=1, replica_groups=mesh['tm'=8,'chan'=32] {'chan'}, use_global_device_ids=true, to_apply=%region_7.7 | all-reduce | flops 256 | bytes 2048 | tf_op jit(solution)/shard_map/while/body/eval_jaxpr/psum | solution.py:89
  1900.8 0.7 broadcast_multiply_fusion.1
  1901.5 64.6 %all-gather.3.cloned.1.call-done = f32[256,1024]{0,1:T(8,128)} async-done(((f32[256,32]{0,1:T(8,128)}), f32[256,1024]{0,1:T(8,128)}) %all-gather.3.cloned.1.call-update) | async-done | bytes 1048592 | tf_op jit(solution)/shard_map/all_gather | solution.py:78
  1966.2 1.9 fusion.1
  1968.2 0.6 copy.21
  (108 shorter events, 3.0 us)
Async XLA Ops:
  6.5 85.7 %reduce-scatter.2.cloned.1.call-start = ((), (), s32[]{:S(2)}) async-start(), calls=%async_computation.1 | async-start | bytes 1179648 | tf_op jit(solution)/shard_map/reduce_scatter | solution.py:59
  6.5 2.9 copy-start.1
  11.5 1.2 copy-start
  152.6 65.7 %all-gather.5.cloned.1.call-start = ((), (), s32[]{:S(2)}) async-start(), calls=%async_computation.3 | async-start | bytes 1081344 | tf_op jit(solution)/shard_map/while/body/eval_jaxpr/all_gather | solution.py:78
  327.5 65.7 %all-gather.5.cloned.1.call-start = ((), (), s32[]{:S(2)}) async-start(), calls=%async_computation.3 | async-start | bytes 1081344 | tf_op jit(solution)/shard_map/while/body/eval_jaxpr/all_gather | solution.py:78
  502.5 65.4 %all-gather.5.cloned.1.call-start = ((), (), s32[]{:S(2)}) async-start(), calls=%async_computation.3 | async-start | bytes 1081344 | tf_op jit(solution)/shard_map/while/body/eval_jaxpr/all_gather | solution.py:78
  677.1 65.4 %all-gather.5.cloned.1.call-start = ((), (), s32[]{:S(2)}) async-start(), calls=%async_computation.3 | async-start | bytes 1081344 | tf_op jit(solution)/shard_map/while/body/eval_jaxpr/all_gather | solution.py:78
  851.7 65.4 %all-gather.5.cloned.1.call-start = ((), (), s32[]{:S(2)}) async-start(), calls=%async_computation.3 | async-start | bytes 1081344 | tf_op jit(solution)/shard_map/while/body/eval_jaxpr/all_gather | solution.py:78
  1026.4 65.7 %all-gather.5.cloned.1.call-start = ((), (), s32[]{:S(2)}) async-start(), calls=%async_computation.3 | async-start | bytes 1081344 | tf_op jit(solution)/shard_map/while/body/eval_jaxpr/all_gather | solution.py:78
  1201.3 65.7 %all-gather.5.cloned.1.call-start = ((), (), s32[]{:S(2)}) async-start(), calls=%async_computation.3 | async-start | bytes 1081344 | tf_op jit(solution)/shard_map/while/body/eval_jaxpr/all_gather | solution.py:78
  1376.2 65.7 %all-gather.5.cloned.1.call-start = ((), (), s32[]{:S(2)}) async-start(), calls=%async_computation.3 | async-start | bytes 1081344 | tf_op jit(solution)/shard_map/while/body/eval_jaxpr/all_gather | solution.py:78
  1551.2 65.4 %all-gather.5.cloned.1.call-start = ((), (), s32[]{:S(2)}) async-start(), calls=%async_computation.3 | async-start | bytes 1081344 | tf_op jit(solution)/shard_map/while/body/eval_jaxpr/all_gather | solution.py:78
  1725.8 65.7 %all-gather.5.cloned.1.call-start = ((), (), s32[]{:S(2)}) async-start(), calls=%async_computation.3 | async-start | bytes 1081344 | tf_op jit(solution)/shard_map/while/body/eval_jaxpr/all_gather | solution.py:78
  1900.8 65.4 %all-gather.3.cloned.1.call-start = ((), (), s32[]{:S(2)}) async-start(), calls=%async_computation.2 | async-start | bytes 1081344 | tf_op jit(solution)/shard_map/all_gather | solution.py:78
Sparse Core Ops, SparseCore 0:
  12.8 79.3 reduce-scatter.1
  155.3 62.9 all-gather.4
  330.2 63.0 all-gather.4
  504.8 63.0 all-gather.4
  679.4 63.0 all-gather.4
  854.1 63.0 all-gather.4
  1029.0 63.0 all-gather.4
  1204.0 63.0 all-gather.4
  1378.9 63.0 all-gather.4
  1553.6 63.0 all-gather.4
  1728.5 62.9 all-gather.4
  1903.1 63.0 all-gather.2
where the time goes:
time: 1980 us
  blocking collectives  1130 us (57%)
  waiting for transfers between devices  792 us (40%)
  matrix products  25.1 us (1%)
    all_gather x11, waiting for transfers between devices, spread_cov(): lax.all_gather(vec, 'chan', axis=1, tiled=True)  713 us
    psum x11, blocking collectives, norm_sum(): return lax.psum(jnp.sum(values, axis=1), 'chan')  601 us
    psum x10, blocking collectives, curv_sum(): return lax.psum(jnp.sum(values, axis=1), 'chan')  526 us
    reduce_scatter x1, waiting for transfers between devices, per_device(): lax.psum_scatter(jnp.concatenate([real_part, imag_part], axis=-1), 'tm',...  78.5 us
  transfers between devices with their start and end apart: 12, of which 12 were waited for; matrix products, arithmetic and copies ran while one was open for 0% of the time, Pallas kernels for 0%

commit v1 on v0

--- a/solution.py
+++ b/solution.py
@@ -6,34 +6,31 @@
 from jax.sharding import PartitionSpec as P
 
 ITERS = 10
-
-
 EPS = 1e-06
 
 
-def conjugate_fill(rows, good, apply_cov, curv_total, norm_total):
+def conjugate_fill(rows, good, cov):
 
-    def operator(vec):
-        return vec + good * apply_cov(good * vec)
+    def apply_cov(vec):
+        return jnp.dot(vec, cov, precision=lax.Precision.HIGHEST, preferred_element_type=jnp.float32)
 
     start = good * rows
-    norm_now = norm_total(start * start)[:, None]
+    norm_now = jnp.sum(start * start, axis=1, keepdims=True)
 
     def advance(step, carry):
         sol, resid, direc, norm_now = carry
-        image = operator(direc)
-        alpha = norm_now / (curv_total(direc * image)[:, None] + EPS)
+        image = direc + good * apply_cov(direc)
+        alpha = norm_now / (jnp.sum(direc * image, axis=1, keepdims=True) + EPS)
         sol = sol + alpha * direc
         resid = resid - alpha * image
-        norm_next = norm_total(resid * resid)[:, None]
+        norm_next = jnp.sum(resid * resid, axis=1, keepdims=True)
         direc = resid + norm_next / (norm_now + EPS) * direc
         return (sol, resid, direc, norm_next)
 
     sol, resid, direc, norm_now = lax.fori_loop(
         0, ITERS, advance, (jnp.zeros_like(rows), start, start, norm_now)
     )
-    signal = apply_cov(good * sol)
-    return good * rows + (1.0 - good) * signal
+    return start + (1.0 - good) * apply_cov(sol)
 
 
 def per_device(vis, beam, fg_cov, flags, m_modes):
@@ -68,30 +65,11 @@
     coeffs = jnp.stack([prods[:, 0, 0] - prods[:, 1, 1], prods[:, 1, 0] + prods[:, 0, 1]], axis=1)
     degrees = coeffs.shape[2]
     good = (1 - flags).astype(jnp.float32)
-    offset = lax.axis_index("chan") * f_dev
-    good_here = lax.dynamic_slice_in_dim(good, offset, f_dev)
-    cov_rows = lax.dynamic_slice_in_dim(fg_cov, offset, f_dev, 0)
     rows = coeffs.reshape(-1, f_dev)
-
-    def spread_cov(vec):
-        return lax.dot_general(
-            lax.all_gather(vec, "chan", axis=1, tiled=True),
-            cov_rows,
-            (((1,), (1,)), ((), ())),
-            precision=lax.Precision.HIGHEST,
-            preferred_element_type=jnp.float32,
-        )
-
-    def curv_sum(values):
-        return lax.psum(jnp.sum(values, axis=1), "chan")
-
-    def norm_sum(values):
-        return lax.psum(jnp.sum(values, axis=1), "chan")
-
-    result = conjugate_fill(rows, good_here, spread_cov, curv_sum, norm_sum).reshape(
-        m_dev, 2, degrees, f_dev
-    )
-    return result
+    mine = lax.all_to_all(rows, "chan", split_axis=0, concat_axis=1, tiled=True)
+    filled = conjugate_fill(mine, good, fg_cov)
+    back = lax.all_to_all(filled, "chan", split_axis=1, concat_axis=0, tiled=True)
+    return back.reshape(m_dev, 2, degrees, f_dev)
 
 
 def solution(mesh):

time: 1980 us -> 190 us (0.10)
  blocking collectives: 1130 us -> 11.3 us
  waiting for transfers between devices: 792 us -> 87.6 us
  matrix products: 25.1 us -> 52.5 us
    psum x21 -> x0, blocking collectives: 1130 us -> none  [the longest x11 601 us: norm_sum(): return lax.psum(jnp.sum(values, axis=1), 'chan')]
    all_gather x11 -> x0, waiting for transfers between devices: 713 us -> none  [spread_cov(): lax.all_gather(vec, 'chan', axis=1, tiled=True)]
    dot_general x11, matrix products: 20.7 us -> 48.2 us  [apply_cov(): jnp.dot(vec, cov, precision=lax.Precision.HIGHEST, preferred_element_type...]
  transfers between devices with their start and end apart: 12 -> 2, of which waited for: 12 -> 2; matrix products, arithmetic and copies ran while one was open for 0% -> 0% of each run, Pallas kernels for 0% -> 0%
where the time goes in v1:
time: 190 us; the launch traced here: 189 us
  waiting for transfers between devices  87.6 us (46%)
  matrix products  52.5 us (28%)
  between operations  13.6 us (7%)
  blocking collectives  11.3 us (6%)
  starting transfers between devices  9.95 us (5%)
  local copies, waits for them, and re-layouts  6.98 us (4%)
  other arithmetic  6.96 us (4%)
    reduce_scatter x1, waiting for transfers between devices, per_device(): lax.psum_scatter(jnp.concatenate([real_part, imag_part], axis=-1), 'tm',...  79.5 us
    dot_general x11, matrix products, apply_cov(): jnp.dot(vec, cov, precision=lax.Precision.HIGHEST, preferred_element_type...  48.2 us
    all_to_all x1, blocking collectives, per_device(): lax.all_to_all(filled, 'chan', split_axis=1, concat_axis=0, tiled=True)  11.3 us
    all_to_all x1, starting transfers between devices, per_device(): mine = lax.all_to_all(rows, 'chan', split_axis=0, concat_axis=1, tiled=True)  9.95 us
    all_to_all x1, waiting for transfers between devices, per_device(): mine = lax.all_to_all(rows, 'chan', split_axis=0, concat_axis=1, tiled=True)  8.03 us
    unnamed x13, local copies, waits for them, and re-layouts  5.09 us
    dot_general x1, matrix products, per_device(): jnp.einsum('mfpln,mfqn->mpqlf', beam, mvis.reshape(m_dev, f_dev, 2, half_...  3.9 us
  transfers between devices with their start and end apart: 2, of which 2 were waited for; matrix products, arithmetic and copies ran while one was open for 0% of the time, Pallas kernels for 0%

profile of v1, /device:TPU:1, one launch (start us, length us, event | category | flops | bytes accessed | tf_op | source)
XLA Modules:
  0.0 189.0 jit_solution(9761023575443789661)
XLA Ops:
  6.5 0.0 reduce-scatter.2.cloned.1.call-start
  6.5 2.8 %copy.17 = bf16[8,8,32,512]{3,1,2,0:T(8,128)(2,1)S(1)} copy(bf16[8,8,32,512]{3,2,1,0:T(8,128)(2,1)} %bitcast.62) | data formatting | bytes 4194304
  9.4 0.1 cosine_convert_fusion
  9.5 0.4 fusion.10
  10.0 0.1 fusion.15
  10.1 0.6 copy.18
  10.7 0.0 copy-start
  10.7 0.6 copy.19
  11.3 0.2 fusion.5
  11.5 1.1 pad_maximum_fusion
  12.7 0.0 reduce-scatter.2.cloned.1.call-update
  12.7 79.5 %reduce-scatter.2.cloned.1.call-done = f32[2,32,512]{2,1,0:T(8,128)} async-done(((f32[16,32,512]{2,1,0:T(8,128)}), f32[2,32,512]{2,1,0:T(8,128)}) %reduce-scatter.2.cloned.1.call-update) | async-done | bytes 131088 | tf_op jit(solution)/shard_map/reduce_scatter | solution.py:56
  92.2 0.9 convert_element_type.12
  93.2 3.9 %convolution_bitcast_fusion = f32[2,2,2,64,32]{3,2,1,4,0:T(2,128)S(1)} fusion(bf16[2,32,2,64,256]{4,3,2,1,0:T(8,128)(2,1)} %param.8, bf16[2,32,2,256,1]{3,2,1,0,4:T(2,128)(2,1)S(1)} %reshape.84), kind=kOutput, calls=%fused_computation.11 | convolution fusion | flops 8388608 | bytes 4325376 | tf_op jit(solution)/shard_map/mfpln,mfqn->mpqlf/dot_general | solution.py:59
  97.1 0.1 fusion.16
  97.2 0.1 copy.10
  97.3 0.7 reshape.86
  98.1 9.9 %all-to-all-start = ((f32[32,1,256]{2,1,0:T(1,128)}), f32[32,1,256]{2,1,0:T(1,128)S(1)}, u32[]{:S(2)}, u32[]{:S(2)}) async-start(f32[32,1,256]{2,1,0:T(1,128)} %reshape.86), calls=%async_computation.1 | async-start | bytes 65536 | tf_op jit(solution)/shard_map/all_to_all | solution.py:69
  108.0 0.1 mul.106
  108.1 8.0 %all-to-all-done = f32[32,1,256]{2,1,0:T(1,128)S(1)} async-done(((f32[32,1,256]{2,1,0:T(1,128)}), f32[32,1,256]{2,1,0:T(1,128)S(1)}, u32[]{:S(2)}, u32[]{:S(2)}) %all-to-all-start) | async-done | bytes 32800 | tf_op jit(solution)/shard_map/all_to_all | solution.py:69
  116.2 0.5 broadcast.53
  116.7 0.7 reduce.1
  117.4 0.1 reshape.87
  117.5 0.1 all_to_all.29
  117.7 0.1 multiply_reduce_fusion.2
  117.8 46.9 %while.17 = (s32[]{:T(128)}, f32[8,1024]{1,0:T(8,128)S(1)}, f32[8,1024]{1,0:T(8,128)S(1)}, f32[8,1024]{1,0:T(8,128)S(1)}, f32[8,1]{0,1:T(1,128)S(1)}, /*index=5*...) while((s32[]{:T(128)}, f32[8,1024]{1,0:T(8,128)S(1)}, f32[8,1024]{1,0:T(8,128)S(1)}, ...), condition=%wide.region_5.6_spmd.clone, body=%wide.region_2.5_spmd.clone.sunk | while | flops 100769808 | bytes 4526599 | solution.py:30
  117.8 4.4 %multiply_reduce_fusion.5 = (f32[8]{0:T(128)S(1)}, f32[8,1024]{1,0:T(8,128)S(1)}) fusion(f32[8,1024]{1,0:T(8,128)S(1)} %get-tuple-element.163, f32[1024,1024]{1,0:T(8,128)} %get-tuple-element.175, f32[1024]{0:T(1024)S(1)} %get-tuple-element.174), kind=kOutput, calls=%fused_computation.6.clone.1 | convolution fusion | flops 100696056 | bytes 4263968 | tf_op jit(solution)/shard_map/while/body/eval_jaxpr/dot_general | solution.py:15
  122.2 0.2 multiply_reduce_fusion.6
  122.4 0.1 multiply_add_fusion.2
  122.5 4.4 %multiply_reduce_fusion.5 = (f32[8]{0:T(128)S(1)}, f32[8,1024]{1,0:T(8,128)S(1)}) fusion(f32[8,1024]{1,0:T(8,128)S(1)} %get-tuple-element.163, f32[1024,1024]{1,0:T(8,128)} %get-tuple-element.175, f32[1024]{0:T(1024)S(1)} %get-tuple-element.174), kind=kOutput, calls=%fused_computation.6.clone.1 | convolution fusion | flops 100696056 | bytes 4263968 | tf_op jit(solution)/shard_map/while/body/eval_jaxpr/dot_general | solution.py:15
  126.9 0.2 multiply_reduce_fusion.6
  127.1 0.1 multiply_add_fusion.2
  127.2 4.4 %multiply_reduce_fusion.5 = (f32[8]{0:T(128)S(1)}, f32[8,1024]{1,0:T(8,128)S(1)}) fusion(f32[8,1024]{1,0:T(8,128)S(1)} %get-tuple-element.163, f32[1024,1024]{1,0:T(8,128)} %get-tuple-element.175, f32[1024]{0:T(1024)S(1)} %get-tuple-element.174), kind=kOutput, calls=%fused_computation.6.clone.1 | convolution fusion | flops 100696056 | bytes 4263968 | tf_op jit(solution)/shard_map/while/body/eval_jaxpr/dot_general | solution.py:15
  131.6 0.2 multiply_reduce_fusion.6
  131.8 0.1 multiply_add_fusion.2
  131.9 4.4 %multiply_reduce_fusion.5 = (f32[8]{0:T(128)S(1)}, f32[8,1024]{1,0:T(8,128)S(1)}) fusion(f32[8,1024]{1,0:T(8,128)S(1)} %get-tuple-element.163, f32[1024,1024]{1,0:T(8,128)} %get-tuple-element.175, f32[1024]{0:T(1024)S(1)} %get-tuple-element.174), kind=kOutput, calls=%fused_computation.6.clone.1 | convolution fusion | flops 100696056 | bytes 4263968 | tf_op jit(solution)/shard_map/while/body/eval_jaxpr/dot_general | solution.py:15
  136.3 0.2 multiply_reduce_fusion.6
  136.5 0.1 multiply_add_fusion.2
  136.6 4.4 %multiply_reduce_fusion.5 = (f32[8]{0:T(128)S(1)}, f32[8,1024]{1,0:T(8,128)S(1)}) fusion(f32[8,1024]{1,0:T(8,128)S(1)} %get-tuple-element.163, f32[1024,1024]{1,0:T(8,128)} %get-tuple-element.175, f32[1024]{0:T(1024)S(1)} %get-tuple-element.174), kind=kOutput, calls=%fused_computation.6.clone.1 | convolution fusion | flops 100696056 | bytes 4263968 | tf_op jit(solution)/shard_map/while/body/eval_jaxpr/dot_general | solution.py:15
  141.0 0.2 multiply_reduce_fusion.6
  141.2 0.1 multiply_add_fusion.2
  141.3 4.4 %multiply_reduce_fusion.5 = (f32[8]{0:T(128)S(1)}, f32[8,1024]{1,0:T(8,128)S(1)}) fusion(f32[8,1024]{1,0:T(8,128)S(1)} %get-tuple-element.163, f32[1024,1024]{1,0:T(8,128)} %get-tuple-element.175, f32[1024]{0:T(1024)S(1)} %get-tuple-element.174), kind=kOutput, calls=%fused_computation.6.clone.1 | convolution fusion | flops 100696056 | bytes 4263968 | tf_op jit(solution)/shard_map/while/body/eval_jaxpr/dot_general | solution.py:15
  145.7 0.2 multiply_reduce_fusion.6
  145.9 0.1 multiply_add_fusion.2
  146.0 4.4 %multiply_reduce_fusion.5 = (f32[8]{0:T(128)S(1)}, f32[8,1024]{1,0:T(8,128)S(1)}) fusion(f32[8,1024]{1,0:T(8,128)S(1)} %get-tuple-element.163, f32[1024,1024]{1,0:T(8,128)} %get-tuple-element.175, f32[1024]{0:T(1024)S(1)} %get-tuple-element.174), kind=kOutput, calls=%fused_computation.6.clone.1 | convolution fusion | flops 100696056 | bytes 4263968 | tf_op jit(solution)/shard_map/while/body/eval_jaxpr/dot_general | solution.py:15
  150.4 0.2 multiply_reduce_fusion.6
  150.6 0.1 multiply_add_fusion.2
  150.7 4.4 %multiply_reduce_fusion.5 = (f32[8]{0:T(128)S(1)}, f32[8,1024]{1,0:T(8,128)S(1)}) fusion(f32[8,1024]{1,0:T(8,128)S(1)} %get-tuple-element.163, f32[1024,1024]{1,0:T(8,128)} %get-tuple-element.175, f32[1024]{0:T(1024)S(1)} %get-tuple-element.174), kind=kOutput, calls=%fused_computation.6.clone.1 | convolution fusion | flops 100696056 | bytes 4263968 | tf_op jit(solution)/shard_map/while/body/eval_jaxpr/dot_general | solution.py:15
  155.1 0.2 multiply_reduce_fusion.6
  155.3 0.1 multiply_add_fusion.2
  155.4 4.4 %multiply_reduce_fusion.5 = (f32[8]{0:T(128)S(1)}, f32[8,1024]{1,0:T(8,128)S(1)}) fusion(f32[8,1024]{1,0:T(8,128)S(1)} %get-tuple-element.163, f32[1024,1024]{1,0:T(8,128)} %get-tuple-element.175, f32[1024]{0:T(1024)S(1)} %get-tuple-element.174), kind=kOutput, calls=%fused_computation.6.clone.1 | convolution fusion | flops 100696056 | bytes 4263968 | tf_op jit(solution)/shard_map/while/body/eval_jaxpr/dot_general | solution.py:15
  159.8 0.2 multiply_reduce_fusion.6
  160.0 0.1 multiply_add_fusion.2
  160.0 4.4 %multiply_reduce_fusion.5 = (f32[8]{0:T(128)S(1)}, f32[8,1024]{1,0:T(8,128)S(1)}) fusion(f32[8,1024]{1,0:T(8,128)S(1)} %get-tuple-element.163, f32[1024,1024]{1,0:T(8,128)} %get-tuple-element.175, f32[1024]{0:T(1024)S(1)} %get-tuple-element.174), kind=kOutput, calls=%fused_computation.6.clone.1 | convolution fusion | flops 100696056 | bytes 4263968 | tf_op jit(solution)/shard_map/while/body/eval_jaxpr/dot_general | solution.py:15
  164.4 0.2 multiply_reduce_fusion.6
  164.7 0.1 multiply_add_fusion.2
  164.7 4.3 %fusion.3 = f32[8,1024]{1,0:T(8,128)S(1)} fusion(f32[8,1024]{1,0:T(8,128)S(1)} %broadcast_multiply_fusion, f32[8,1024]{1,0:T(8,128)S(1)} %get-tuple-element.42, f32[1024,1024]{1,0:T(8,128)} %get-tuple-element.179, f32[1024]{0:T(1024)S(1)} %broadcast_subtract_fusion), kind=kOutput, calls=%fused_computation.13 | convolution fusion | flops 100679680 | bytes 4296704 | tf_op jit(solution)/shard_map/dot_general | solution.py:15
  169.0 0.1 all_to_all.30
  169.1 0.1 copy.21
  169.2 0.1 reshape.88
  169.3 11.3 %all_to_all.35 = f32[32,1,256]{2,1,0:T(1,128)S(1)} all-to-all(f32[32,1,256]{2,1,0:T(1,128)S(1)} %reshape.88), channel_id=1, replica_groups=mesh['tm'=8,'chan'=32] {'chan'}, dimensions={0} | all-to-all | bytes 65536 | tf_op jit(solution)/shard_map/all_to_all | solution.py:71
  180.6 0.7 reduce.2
  181.3 0.1 reshape.89
  181.4 0.7 copy.13
  (44 shorter events, 0.3 us)
Async XLA Ops:
  6.5 2.9 %copy-start.1 = (s32[16]{0:T(128)S(1)}, s32[16]{0:T(128)}, u32[]{:S(2)}) copy-start(s32[16]{0:T(128)} %param.11) | copy-start | bytes 196
  6.5 85.7 %reduce-scatter.2.cloned.1.call-start = ((), (), s32[]{:S(2)}) async-start(), calls=%async_computation.3 | async-start | bytes 1179648 | tf_op jit(solution)/shard_map/reduce_scatter | solution.py:56
  10.7 2.0 %copy-start = (s32[1024]{0:T(1024)S(1)}, s32[1024]{0:T(1024)}, u32[]{:S(2)}) copy-start(s32[1024]{0:T(1024)} %param.10) | copy-start | bytes 12292
  98.1 18.1 %all-to-all-start = ((f32[32,1,256]{2,1,0:T(1,128)}), f32[32,1,256]{2,1,0:T(1,128)S(1)}, u32[]{:S(2)}, u32[]{:S(2)}) async-start(f32[32,1,256]{2,1,0:T(1,128)} %reshape.86), calls=%async_computation.1 | async-start | bytes 65536 | tf_op jit(solution)/shard_map/all_to_all | solution.py:69
Sparse Core Ops, SparseCore 0:
  12.8 79.3 reduce-scatter.1

commit v2 on v1

v2 whole, which is shorter than its diff:
```python
import functools
import math

import jax
import jax.numpy as jnp
from jax import lax
from jax.experimental import pallas as pl
from jax.experimental.pallas import tpu as pltpu
from jax.sharding import PartitionSpec as P

ITERS = 10
EPS = 1e-06
MESH = pl.DeviceIdType.MESH


def swap_groups(tiles):
    sub = lax.broadcasted_iota(jnp.int32, (8, 128), 0)
    lane = lax.broadcasted_iota(jnp.int32, (8, 128), 1)
    s1, l1 = (sub >= 4), (lane >= 64)
    s0, l0 = (sub % 4 >= 2), (lane % 64 >= 32)
    done = []
    for x in tiles:
        moved = pltpu.roll(pltpu.roll(x, 4, 0), 64, 1)
        x = jnp.where(s1 == l1, x, moved)
        up = pltpu.roll(pltpu.roll(x, 6, 0), 32, 1)
        down = pltpu.roll(pltpu.roll(x, 2, 0), 96, 1)
        x = jnp.where(s0 == l0, x, jnp.where(l0, up, down))
        done.append(x)
    return done


def kernel(
    n_tm, n_chan, m_ref, flags_ref, vis_hbm, beam_hbm, cov_hbm, out_ref,
    vis_v, beam_v, cov_v, pair_v, kron_v, part_v, got_v, give1, take1, give2, take2,
    local_sem, psend, precv, send1, recv1, send2, recv2,
):
    t_dev, f_dev, width = vis_v.shape
    half_w = width // 2
    n_m = m_ref.shape[0]
    m_dev = n_m // n_tm
    n_time = t_dev * n_tm
    fh = f_dev // 2
    n_f = cov_v.shape[0]
    my_tm = lax.axis_index("tm")
    my_chan = lax.axis_index("chan")

    barrier = pltpu.get_barrier_semaphore()
    for i in range(1, n_tm):
        pl.semaphore_signal(barrier, inc=1, device_id={"tm": lax.rem(my_tm + i, n_tm)}, device_id_type=MESH)

    @pl.loop(1, n_chan)
    def _(i):
        pl.semaphore_signal(barrier, inc=1, device_id={"chan": lax.rem(my_chan + i, n_chan)}, device_id_type=MESH)

    vis_copies = [
        pltpu.make_async_copy(
            vis_hbm.at[:, pl.ds(h * fh, fh), :], vis_v.at[:, pl.ds(h * fh, fh), :], local_sem.at[h]
        )
        for h in range(2)
    ]
    for copy in vis_copies:
        copy.start()

    row = lax.broadcasted_iota(jnp.int32, (n_m, t_dev), 0)
    modes = jnp.zeros((n_m, t_dev), jnp.int32)
    for k in range(n_m):
        modes = jnp.where(row == k, m_ref[k], modes)
    times = my_tm * t_dev + lax.broadcasted_iota(jnp.int32, (n_m, t_dev), 1)
    index = lax.rem(modes * times, n_time)
    angle = 2.0 * math.pi / n_time * index.astype(jnp.float32)
    wide = t_dev * fh
    spread = (
        lax.broadcasted_iota(jnp.int32, (t_dev, wide), 1) // fh == lax.broadcasted_iota(jnp.int32, (t_dev, wide), 0)
    ).astype(jnp.float32).astype(jnp.bfloat16)
    same = lax.broadcasted_iota(jnp.int32, (fh, wide), 1) % fh == lax.broadcasted_iota(jnp.int32, (fh, wide), 0)
    for q, table in enumerate((jnp.cos(angle), jnp.sin(angle))):
        lanes = jnp.dot(table.astype(jnp.bfloat16), spread, preferred_element_type=jnp.float32)
        for k in range(n_m):
            kron_v[q, k * fh : (k + 1) * fh, :] = jnp.where(same, lanes[k : k + 1, :], 0.0).astype(jnp.bfloat16)

    scale = 1.0 / math.sqrt(n_time)
    part_copies = []
    for h in range(2):
        vis_copies[h].wait()
        if h == 1:
            beam_copy = pltpu.make_async_copy(beam_hbm, beam_v, local_sem.at[2])
            cov_copy = pltpu.make_async_copy(cov_hbm, cov_v, local_sem.at[3])
            cov_copy.start()
            beam_copy.start()
        data = vis_v[:, h * fh : (h + 1) * fh, :].reshape(t_dev * fh, width)
        c = jnp.dot(kron_v[0], data, preferred_element_type=jnp.float32)
        s = jnp.dot(kron_v[1], data, preferred_element_type=jnp.float32)
        real = (c[:, :half_w] + s[:, half_w:]) * scale
        imag = (c[:, half_w:] - s[:, :half_w]) * scale
        part_v[:, h, :, :half_w] = real.reshape(n_tm, m_dev * fh, half_w)
        part_v[:, h, :, half_w:] = imag.reshape(n_tm, m_dev * fh, half_w)
        if h == 0:
            pl.semaphore_wait(barrier, n_tm - 1 + n_chan - 1)
        for i in range(1, n_tm):
            owner = lax.rem(my_tm + i, n_tm)
            copy = pltpu.make_async_remote_copy(
                src_ref=part_v.at[owner, h], dst_ref=got_v.at[i - 1, h],
                send_sem=psend.at[i - 1, h], recv_sem=precv.at[i - 1, h],
                device_id={"tm": owner}, device_id_type=MESH,
            )
            copy.start()
            part_copies.append(copy)

    cov_copy.wait()
    step = 64

    @pl.loop(0, n_f // step)
    def _(j):
        rows = pl.ds(pl.multiple_of(j * step, step), step)
        low_rows = pl.ds(pl.multiple_of(n_f + j * step, step), step)
        block = cov_v[rows, :]
        high = block.astype(jnp.bfloat16)
        pair_v[rows, :] = high
        pair_v[low_rows, :] = (block - high.astype(jnp.float32)).astype(jnp.bfloat16)

    beam_copy.wait()
    for copy in part_copies:
        copy.wait_recv()
    pieces = {}
    for h in range(2):
        total = part_v[my_tm, h]
        for i in range(n_tm - 1):
            total = total + got_v[i, h]
        mvis = total.astype(jnp.bfloat16).astype(jnp.float32)
        for m in range(m_dev):
            block = mvis[m * fh : (m + 1) * fh, :]
            pieces[(m, 0, h)] = block[:, :half_w]
            pieces[(m, 1, h)] = block[:, half_w:]
    against_real, against_imag = [], []
    for m in range(m_dev):
        for p in range(2):
            for h in range(2):
                against_real.append(pieces[(m, p, h)])
                against_imag.append(-pieces[(m, 1, h)] if p == 0 else pieces[(m, 0, h)])
    weights = jnp.concatenate(
        [jnp.concatenate(against_real, axis=0).T, jnp.concatenate(against_imag, axis=0).T], axis=0
    ).astype(jnp.bfloat16)

    degrees = beam_v.shape[3]
    lanes = 2 * m_dev * f_dev
    lane = lax.broadcasted_iota(jnp.int32, (degrees, lanes), 1)
    lane_id = lane // (2 * f_dev) * f_dev + lane % f_dev
    take = 4
    per_m = f_dev // take

    def project(j, acc):
        m = j // per_m
        f0 = (j - m * per_m) * take
        lhs = jnp.concatenate(
            [
                beam_v[m, pl.ds(f0, take), 0].reshape(take * degrees, half_w),
                beam_v[m, pl.ds(f0, take), 1].reshape(take * degrees, half_w),
            ],
            axis=1,
        )
        prod = jnp.dot(lhs, weights, preferred_element_type=jnp.float32)
        for i in range(take):
            acc = jnp.where(lane_id == m * f_dev + f0 + i, prod[i * degrees : (i + 1) * degrees, :], acc)
        return acc

    coeffs = lax.fori_loop(0, m_dev * per_m, project, jnp.zeros((degrees, lanes), jnp.float32))
    pair = degrees // n_chan
    give1[...] = coeffs.reshape(n_chan, pair, lanes)

    def exchange(give, got, ssem, rsem):
        def remote(i):
            peer = lax.rem(my_chan + i, n_chan)
            return pltpu.make_async_remote_copy(
                src_ref=give.at[peer], dst_ref=got.at[my_chan], send_sem=ssem.at[i], recv_sem=rsem.at[i],
                device_id={"chan": peer}, device_id_type=MESH,
            )

        @pl.loop(1, n_chan)
        def _(i):
            remote(i).start()

        own = pltpu.make_async_copy(give.at[my_chan], got.at[my_chan], ssem.at[0])
        own.start()
        own.wait()

        @pl.loop(1, n_chan)
        def _(i):
            remote(i).wait_recv()

    exchange(give1, take1, send1, recv1)
    mixed = take1[...].reshape(degrees, lanes)
    n_tiles = degrees // 8
    data = jnp.concatenate(swap_groups([mixed[8 * j : 8 * j + 8, :] for j in range(n_tiles)]), axis=1)
    good = jnp.broadcast_to((1 - flags_ref[...]).astype(jnp.float32), (8, n_f))

    def apply_cov(vec):
        high = vec.astype(jnp.bfloat16).astype(jnp.float32)
        both = jnp.concatenate([high, vec - high], axis=0).astype(jnp.bfloat16)
        prod = jnp.dot(jnp.concatenate([both, both], axis=1), pair_v[...], preferred_element_type=jnp.float32)
        return prod[:8, :] + prod[8:, :]

    def total_of(values):
        return jnp.sum(values, axis=1, keepdims=True)

    start = good * data

    def advance(step, carry):
        sol, resid, direc, norm_now = carry
        image = direc + good * apply_cov(direc)
        alpha = norm_now / (total_of(direc * image) + EPS)
        sol = sol + alpha * direc
        resid = resid - alpha * image
        norm_next = total_of(resid * resid)
        direc = resid + norm_next / (norm_now + EPS) * direc
        return (sol, resid, direc, norm_next)

    sol, _, _, _ = lax.fori_loop(0, ITERS, advance, (jnp.zeros_like(start), start, start, total_of(start * start)))
    filled = start + (1.0 - good) * apply_cov(sol)
    tiles = swap_groups([filled[:, 128 * j : 128 * (j + 1)] for j in range(n_tiles)])
    give2[...] = jnp.concatenate(tiles, axis=0).reshape(n_chan, pair, lanes)
    exchange(give2, take2, send2, recv2)
    back = take2[...].reshape(degrees, lanes)
    for m in range(m_dev):
        for p in range(2):
            at = (2 * m + p) * f_dev
            out_ref[m, p] = back[:, at : at + f_dev]

    for copy in part_copies:
        copy.wait_send()
    for give, got, ssem, rsem in ((give1, take1, send1, recv1), (give2, take2, send2, recv2)):

        @pl.loop(1, n_chan)
        def _(i):
            peer = lax.rem(my_chan + i, n_chan)
            pltpu.make_async_remote_copy(
                src_ref=give.at[peer], dst_ref=got.at[my_chan], send_sem=ssem.at[i], recv_sem=rsem.at[i],
                device_id={"chan": peer}, device_id_type=MESH,
            ).wait_send()


def per_device(n_tm, n_chan, vis, beam, fg_cov, flags, m_modes):
    t_dev, f_dev, width = vis.shape
    m_dev, _, _, degrees, half_w = beam.shape
    n_f = fg_cov.shape[0]
    lanes = 2 * m_dev * f_dev
    block = (n_chan, degrees // n_chan, lanes)
    any_space = pl.BlockSpec(memory_space=pl.ANY)
    return pl.pallas_call(
        functools.partial(kernel, n_tm, n_chan),
        out_shape=jax.ShapeDtypeStruct((m_dev, 2, degrees, f_dev), jnp.float32),
        in_specs=[
            pl.BlockSpec(memory_space=pltpu.SMEM),
            pl.BlockSpec(memory_space=pltpu.VMEM),
            any_space,
            any_space,
            any_space,
        ],
        out_specs=pl.BlockSpec(memory_space=pltpu.VMEM),
        scratch_shapes=[
            pltpu.VMEM(vis.shape, vis.dtype),
            pltpu.VMEM(beam.shape, beam.dtype),
            pltpu.VMEM(fg_cov.shape, jnp.float32),
            pltpu.VMEM((2 * n_f, n_f), jnp.bfloat16),
            pltpu.VMEM((2, m_dev * n_tm * f_dev // 2, t_dev * f_dev // 2), jnp.bfloat16),
            pltpu.VMEM((n_tm, 2, m_dev * f_dev // 2, width), jnp.float32),
            pltpu.VMEM((n_tm - 1, 2, m_dev * f_dev // 2, width), jnp.float32),
            pltpu.VMEM(block, jnp.float32),
            pltpu.VMEM(block, jnp.float32),
            pltpu.VMEM(block, jnp.float32),
            pltpu.VMEM(block, jnp.float32),
            pltpu.SemaphoreType.DMA((4,)),
            pltpu.SemaphoreType.DMA((n_tm - 1, 2)),
            pltpu.SemaphoreType.DMA((n_tm - 1, 2)),
            pltpu.SemaphoreType.DMA((n_chan,)),
            pltpu.SemaphoreType.DMA((n_chan,)),
            pltpu.SemaphoreType.DMA((n_chan,)),
            pltpu.SemaphoreType.DMA((n_chan,)),
        ],
        compiler_params=pltpu.CompilerParams(
            collective_id=0, has_side_effects=True, vmem_limit_bytes=48 * 1024 * 1024
        ),
    )(m_modes, flags.reshape(1, n_f), vis, beam, fg_cov)


def solution(mesh):
    placed = (P("tm", "chan", None), P("tm", "chan", None, None, None), P(), P(), P())
    return jax.shard_map(
        functools.partial(per_device, mesh.shape["tm"], mesh.shape["chan"]),
        mesh=mesh,
        in_specs=placed,
        out_specs=P("tm", None, None, "chan"),
        check_vma=False,
    )
```

time: 190 us -> 54.8 us (0.29)
  waiting for transfers between devices: 87.6 us -> 0 us
  matrix products: 52.5 us -> 0 us
  Pallas kernels: 0 us -> 50.9 us
  between operations: 13.6 us -> 0.01 us
  blocking collectives: 11.3 us -> 0 us
  starting transfers between devices: 9.95 us -> 0 us
  other arithmetic: 6.96 us -> 0 us
  local copies, waits for them, and re-layouts: 6.98 us -> 3.65 us
    reduce_scatter x1 -> x0, waiting for transfers between devices: 79.5 us -> none  [per_device(): lax.psum_scatter(jnp.concatenate([real_part, imag_part], axis=-1), 'tm',...]
    dot_general x13 -> x0, matrix products: 52.5 us -> none  [the longest x11 48.2 us: apply_cov(): jnp.dot(vec, cov, precision=lax.Precision.HIGHEST, preferred_element_type...]
    pallas_call x0 -> x1, Pallas kernels: none -> 50.9 us  [per_device(): pl.pallas_call(functools.partial(kernel, n_tm, n_chan), out_shape=jax.Sha...]
    all_to_all x1 -> x0, blocking collectives: 11.3 us -> none  [per_device(): lax.all_to_all(filled, 'chan', split_axis=1, concat_axis=0, tiled=True)]
    all_to_all x1 -> x0, starting transfers between devices: 9.95 us -> none  [per_device(): mine = lax.all_to_all(rows, 'chan', split_axis=0, concat_axis=1, tiled=True)]
    all_to_all x1 -> x0, waiting for transfers between devices: 8.03 us -> none  [per_device(): mine = lax.all_to_all(rows, 'chan', split_axis=0, concat_axis=1, tiled=True)]
    unnamed x13 -> x6, local copies, waits for them, and re-layouts: 5.09 us -> 2.93 us
    reduce_sum x11 -> x0, other arithmetic: 2.09 us -> none  [the longest x10 1.94 us: advance(): norm_next = jnp.sum(resid * resid, axis=1, keepdims=True)]
  transfers between devices with their start and end apart: 2 -> 0, of which waited for: 2 -> 0; matrix products, arithmetic and copies ran while one was open for 0% -> 0% of each run, Pallas kernels for 0% -> 0%
where the time goes in v2:
time: 54.8 us; the launch traced here: 54.5 us
  Pallas kernels  50.9 us (93%)
  local copies, waits for them, and re-layouts  3.65 us (7%)
    pallas_call x1, Pallas kernels, per_device(): pl.pallas_call(functools.partial(kernel, n_tm, n_chan), out_shape=jax.Sha...  50.9 us
    unnamed x6, local copies, waits for them, and re-layouts  2.93 us

profile of v2, /device:TPU:1, one launch (start us, length us, event | category | flops | bytes accessed | tf_op | source)
XLA Modules:
  0.0 54.5 jit_solution(16409803120897186337)
XLA Ops:
  0.0 0.0 copy-start
  0.0 1.6 %copy-done = bf16[64,32,512]{2,1,0:T(8,128)(2,1)S(1)} copy-done((bf16[64,32,512]{2,1,0:T(8,128)(2,1)S(1)}, bf16[64,32,512]{2,1,0:T(8,128)(2,1)}, u32[]{:S(2)}) %copy-start) | copy-done | bytes 2097176
  1.6 0.0 copy-start.1
  1.6 0.7 %copy-done.1 = s32[1024]{0:T(1024)S(1)} copy-done((s32[1024]{0:T(1024)S(1)}, s32[1024]{0:T(1024)}, u32[]{:S(2)}) %copy-start.1) | copy-done | bytes 4120
  2.3 0.0 copy-start.2
  2.3 0.7 %copy-done.2 = s32[16]{0:T(128)S(1)} copy-done((s32[16]{0:T(128)S(1)}, s32[16]{0:T(128)}, u32[]{:S(2)}) %copy-start.2) | copy-done | bytes 88
  2.9 50.9 %shard_map.55 = f32[2,2,64,32]{3,2,1,0:T(8,128)S(1)} custom-call(s32[16]{0:T(128)S(1)} %copy-done.2, s32[1,1024]{1,0:T(1,128)S(1)} %bitcast.1, bf16[64,32,512]{2,1,0:T(8,128)(2,1)S(1)} %copy-done, bf16[2,32,2,64,256]{4,3,2,1,0:T(8,128)(2,1)} %beam_hbm.1, f32[1024,1024]{1,0:T(8,128)} %cov_hbm.1), custom_call_target="tpu_custom_call" | custom-call | tf_op jit(solution)/shard_map/pallas_call | solution.py:248
  53.8 0.7 %copy.6 = f32[2,2,64,32]{2,3,1,0:T(8,128)} copy(f32[2,2,64,32]{3,2,1,0:T(8,128)S(1)} %shard_map.55) | data formatting | bytes 65536 | tf_op jit(solution)/shard_map/pallas_call | solution.py:248
Async XLA Ops:
  0.0 1.6 %copy-start = (bf16[64,32,512]{2,1,0:T(8,128)(2,1)S(1)}, bf16[64,32,512]{2,1,0:T(8,128)(2,1)}, u32[]{:S(2)}) copy-start(bf16[64,32,512]{2,1,0:T(8,128)(2,1)} %vis_hbm.1) | copy-start | bytes 6291460
  1.6 0.7 %copy-start.1 = (s32[1024]{0:T(1024)S(1)}, s32[1024]{0:T(1024)}, u32[]{:S(2)}) copy-start(s32[1024]{0:T(1024)} %param.8) | copy-start | bytes 12292
  2.3 0.7 %copy-start.2 = (s32[16]{0:T(128)S(1)}, s32[16]{0:T(128)}, u32[]{:S(2)}) copy-start(s32[16]{0:T(128)} %m_ref.1) | copy-start | bytes 196

commit v3 on v2

v3 whole, which is shorter than its diff:
```python
import functools
import math

import jax
import jax.numpy as jnp
from jax import lax
from jax.experimental import pallas as pl
from jax.experimental.pallas import tpu as pltpu
from jax.sharding import PartitionSpec as P

ITERS = 10
EPS = 1e-06
MESH = pl.DeviceIdType.MESH


def swap_groups(tiles):
    sub = lax.broadcasted_iota(jnp.int32, (8, 128), 0)
    lane = lax.broadcasted_iota(jnp.int32, (8, 128), 1)
    s1, l1 = (sub >= 4), (lane >= 64)
    s0, l0 = (sub % 4 >= 2), (lane % 64 >= 32)
    done = []
    for x in tiles:
        moved = pltpu.roll(pltpu.roll(x, 4, 0), 64, 1)
        x = jnp.where(s1 == l1, x, moved)
        up = pltpu.roll(pltpu.roll(x, 6, 0), 32, 1)
        down = pltpu.roll(pltpu.roll(x, 2, 0), 96, 1)
        x = jnp.where(s0 == l0, x, jnp.where(l0, up, down))
        done.append(x)
    return done


def kernel(
    n_tm, n_chan, m_hbm, flags_hbm, vis_hbm, beam_hbm, cov_hbm, out_ref,
    m_ref, flags_ref, vis_v, beam_v, cov_v, pair_v, kron_v, part_v, got_v, give1, take1, give2, take2,
    local_sem, psend, precv, send1, recv1, send2, recv2,
):
    t_dev, f_dev, width = vis_v.shape
    half_w = width // 2
    n_m = m_ref.shape[0]
    m_dev = n_m // n_tm
    n_time = t_dev * n_tm
    fh = f_dev // 2
    n_f = cov_v.shape[0]
    my_tm = lax.axis_index("tm")
    my_chan = lax.axis_index("chan")

    modes_copy = pltpu.make_async_copy(m_hbm, m_ref, local_sem.at[4])
    modes_copy.start()
    vis_copies = [
        pltpu.make_async_copy(
            vis_hbm.at[:, pl.ds(h * fh, fh), :], vis_v.at[:, pl.ds(h * fh, fh), :], local_sem.at[h]
        )
        for h in range(2)
    ]
    for copy in vis_copies:
        copy.start()
    flags_copy = pltpu.make_async_copy(flags_hbm, flags_ref, local_sem.at[5])
    flags_copy.start()

    barrier = pltpu.get_barrier_semaphore()
    for i in range(1, n_tm):
        pl.semaphore_signal(barrier, inc=1, device_id={"tm": lax.rem(my_tm + i, n_tm)}, device_id_type=MESH)
    for i in range(1, n_chan):
        pl.semaphore_signal(barrier, inc=1, device_id={"chan": lax.rem(my_chan + i, n_chan)}, device_id_type=MESH)

    modes_copy.wait()
    row = lax.broadcasted_iota(jnp.int32, (n_m, t_dev), 0)
    modes = jnp.zeros((n_m, t_dev), jnp.int32)
    for k in range(n_m):
        modes = jnp.where(row == k, m_ref[k], modes)
    times = my_tm * t_dev + lax.broadcasted_iota(jnp.int32, (n_m, t_dev), 1)
    index = lax.rem(modes * times, n_time)
    angle = 2.0 * math.pi / n_time * index.astype(jnp.float32)
    wide = t_dev * fh
    spread = (
        lax.broadcasted_iota(jnp.int32, (t_dev, wide), 1) // fh == lax.broadcasted_iota(jnp.int32, (t_dev, wide), 0)
    ).astype(jnp.float32).astype(jnp.bfloat16)
    same = lax.broadcasted_iota(jnp.int32, (fh, wide), 1) % fh == lax.broadcasted_iota(jnp.int32, (fh, wide), 0)
    for q, table in enumerate((jnp.cos(angle), jnp.sin(angle))):
        lanes = jnp.dot(table.astype(jnp.bfloat16), spread, preferred_element_type=jnp.float32)
        for k in range(n_m):
            kron_v[q, k * fh : (k + 1) * fh, :] = jnp.where(same, lanes[k : k + 1, :], 0.0).astype(jnp.bfloat16)

    scale = 1.0 / math.sqrt(n_time)
    part_copies = ([], [])
    for h in range(2):
        vis_copies[h].wait()
        if h == 1:
            beam_copy = pltpu.make_async_copy(beam_hbm, beam_v, local_sem.at[2])
            cov_copy = pltpu.make_async_copy(cov_hbm, cov_v, local_sem.at[3])
            cov_copy.start()
            beam_copy.start()
        data = vis_v[:, h * fh : (h + 1) * fh, :].reshape(t_dev * fh, width)
        c = jnp.dot(kron_v[0], data, preferred_element_type=jnp.float32)
        s = jnp.dot(kron_v[1], data, preferred_element_type=jnp.float32)
        real = (c[:, :half_w] + s[:, half_w:]) * scale
        imag = (c[:, half_w:] - s[:, :half_w]) * scale
        part_v[:, h, :, :half_w] = real.reshape(n_tm, m_dev * fh, half_w)
        part_v[:, h, :, half_w:] = imag.reshape(n_tm, m_dev * fh, half_w)
        if h == 0:
            pl.semaphore_wait(barrier, n_tm - 1 + n_chan - 1)
        for i in range(1, n_tm):
            owner = lax.rem(my_tm + i, n_tm)
            copy = pltpu.make_async_remote_copy(
                src_ref=part_v.at[owner, h], dst_ref=got_v.at[i - 1, h],
                send_sem=psend.at[i - 1, h], recv_sem=precv.at[i - 1, h],
                device_id={"tm": owner}, device_id_type=MESH,
            )
            copy.start()
            part_copies[h].append(copy)

    cov_copy.wait()
    step = 64

    @pl.loop(0, n_f // step)
    def _(j):
        rows = pl.ds(pl.multiple_of(j * step, step), step)
        low_rows = pl.ds(pl.multiple_of(n_f + j * step, step), step)
        block = cov_v[rows, :]
        high = block.astype(jnp.bfloat16)
        pair_v[rows, :] = high
        pair_v[low_rows, :] = (block - high.astype(jnp.float32)).astype(jnp.bfloat16)

    beam_copy.wait()
    degrees = beam_v.shape[3]
    lanes = 2 * m_dev * f_dev
    lane = lax.broadcasted_iota(jnp.int32, (degrees, lanes), 1)
    lane_id = lane // (2 * f_dev) * f_dev + lane % f_dev
    coeffs = jnp.zeros((degrees, lanes), jnp.float32)
    blank = jnp.zeros((fh, half_w), jnp.float32)
    for h in range(2):
        for copy in part_copies[h]:
            copy.wait_recv()
        total = part_v[my_tm, h]
        for i in range(n_tm - 1):
            total = total + got_v[i, h]
        mvis = total.astype(jnp.bfloat16).astype(jnp.float32)
        against_real, against_imag = [], []
        for m in range(m_dev):
            block = mvis[m * fh : (m + 1) * fh, :]
            re, im = block[:, :half_w], block[:, half_w:]
            for first, second in ((re, -im), (im, re)):
                against_real += [first, blank] if h == 0 else [blank, first]
                against_imag += [second, blank] if h == 0 else [blank, second]
        weights = jnp.concatenate(
            [jnp.concatenate(against_real, axis=0).T, jnp.concatenate(against_imag, axis=0).T], axis=0
        ).astype(jnp.bfloat16)
        for m in range(m_dev):
            rows = slice(h * fh, (h + 1) * fh)
            lhs = jnp.concatenate(
                [
                    beam_v[m, rows, 0].reshape(fh * degrees, half_w),
                    beam_v[m, rows, 1].reshape(fh * degrees, half_w),
                ],
                axis=1,
            )
            prod = jnp.dot(lhs, weights, preferred_element_type=jnp.float32)
            for i in range(fh):
                coeffs = jnp.where(
                    lane_id == m * f_dev + h * fh + i, prod[i * degrees : (i + 1) * degrees, :], coeffs
                )
    pair = degrees // n_chan
    give1[...] = coeffs.reshape(n_chan, pair, lanes)

    order = [n_chan // 2]
    for i in range(1, n_chan // 2):
        order += [n_chan // 2 - i, n_chan // 2 + i]

    def exchange(give, got, ssem, rsem):
        got[my_chan] = give[my_chan]
        for i in order:
            peer = lax.rem(my_chan + i, n_chan)
            pltpu.make_async_remote_copy(
                src_ref=give.at[peer], dst_ref=got.at[my_chan], send_sem=ssem.at[0], recv_sem=rsem.at[0],
                device_id={"chan": peer}, device_id_type=MESH,
            ).start()

    def wait_all(buf, sem):
        others = buf.at[pl.ds(0, n_chan - 1)]
        pltpu.make_async_copy(others, others, sem.at[0]).wait()

    exchange(give1, take1, send1, recv1)
    flags_copy.wait()
    wait_all(take1, recv1)
    mixed = take1[...].reshape(degrees, lanes)
    n_tiles = degrees // 8
    data = jnp.concatenate(swap_groups([mixed[8 * j : 8 * j + 8, :] for j in range(n_tiles)]), axis=1)
    good = jnp.broadcast_to((1 - flags_ref[...]).astype(jnp.float32), (8, n_f))

    def apply_cov(vec):
        high = vec.astype(jnp.bfloat16).astype(jnp.float32)
        both = jnp.concatenate([high, vec - high], axis=0).astype(jnp.bfloat16)
        prod = jnp.dot(jnp.concatenate([both, both], axis=1), pair_v[...], preferred_element_type=jnp.float32)
        return prod[:8, :] + prod[8:, :]

    def total_of(values):
        return jnp.sum(values, axis=1, keepdims=True)

    start = good * data

    def advance(step, carry):
        signal, resid, direc, norm_now = carry
        spread_out = apply_cov(direc)
        image = direc + good * spread_out
        alpha = norm_now / (total_of(direc * image) + EPS)
        signal = signal + alpha * spread_out
        resid = resid - alpha * image
        norm_next = total_of(resid * resid)
        direc = resid + norm_next / (norm_now + EPS) * direc
        return (signal, resid, direc, norm_next)

    signal, _, direc, norm_now = lax.fori_loop(
        0, ITERS - 1, advance, (jnp.zeros_like(start), start, start, total_of(start * start))
    )
    spread_out = apply_cov(direc)
    alpha = norm_now / (total_of(direc * (direc + good * spread_out)) + EPS)
    filled = start + (1.0 - good) * (signal + alpha * spread_out)
    tiles = swap_groups([filled[:, 128 * j : 128 * (j + 1)] for j in range(n_tiles)])
    give2[...] = jnp.concatenate(tiles, axis=0).reshape(n_chan, pair, lanes)
    exchange(give2, take2, send2, recv2)
    for copies in part_copies:
        for copy in copies:
            copy.wait_send()
    wait_all(give1, send1)
    wait_all(take2, recv2)
    back = take2[...].reshape(degrees, lanes)
    out_ref[...] = back.T.reshape(m_dev, 2, f_dev, degrees)
    wait_all(give2, send2)


def per_device(n_tm, n_chan, vis, beam, fg_cov, flags, m_modes):
    t_dev, f_dev, width = vis.shape
    m_dev, _, _, degrees, half_w = beam.shape
    n_f = fg_cov.shape[0]
    lanes = 2 * m_dev * f_dev
    block = (n_chan, degrees // n_chan, lanes)
    hbm = pl.BlockSpec(memory_space=pltpu.HBM)
    filled = pl.pallas_call(
        functools.partial(kernel, n_tm, n_chan),
        out_shape=jax.ShapeDtypeStruct((m_dev, 2, f_dev, degrees), jnp.float32),
        in_specs=[hbm] * 5,
        out_specs=pl.BlockSpec(memory_space=pltpu.VMEM),
        scratch_shapes=[
            pltpu.SMEM(m_modes.shape, jnp.int32),
            pltpu.VMEM((1, n_f), jnp.int32),
            pltpu.VMEM(vis.shape, vis.dtype),
            pltpu.VMEM(beam.shape, beam.dtype),
            pltpu.VMEM(fg_cov.shape, jnp.float32),
            pltpu.VMEM((2 * n_f, n_f), jnp.bfloat16),
            pltpu.VMEM((2, m_dev * n_tm * f_dev // 2, t_dev * f_dev // 2), jnp.bfloat16),
            pltpu.VMEM((n_tm, 2, m_dev * f_dev // 2, width), jnp.float32),
            pltpu.VMEM((n_tm - 1, 2, m_dev * f_dev // 2, width), jnp.float32),
            pltpu.VMEM(block, jnp.float32),
            pltpu.VMEM(block, jnp.float32),
            pltpu.VMEM(block, jnp.float32),
            pltpu.VMEM(block, jnp.float32),
            pltpu.SemaphoreType.DMA((6,)),
            pltpu.SemaphoreType.DMA((n_tm - 1, 2)),
            pltpu.SemaphoreType.DMA((n_tm - 1, 2)),
            pltpu.SemaphoreType.DMA((1,)),
            pltpu.SemaphoreType.DMA((1,)),
            pltpu.SemaphoreType.DMA((1,)),
            pltpu.SemaphoreType.DMA((1,)),
        ],
        compiler_params=pltpu.CompilerParams(
            collective_id=0, has_side_effects=True, vmem_limit_bytes=48 * 1024 * 1024
        ),
    )(*[pltpu.with_memory_space_constraint(a, pltpu.HBM) for a in (m_modes, flags.reshape(1, n_f), vis, beam, fg_cov)])
    return jnp.transpose(filled, (0, 1, 3, 2))


def solution(mesh):
    placed = (P("tm", "chan", None), P("tm", "chan", None, None, None), P(), P(), P())
    return jax.shard_map(
        functools.partial(per_device, mesh.shape["tm"], mesh.shape["chan"]),
        mesh=mesh,
        in_specs=placed,
        out_specs=P("tm", None, None, "chan"),
        check_vma=False,
    )
```

time: 54.8 us -> 45.1 us (0.82)
  Pallas kernels: 50.9 us -> 44.3 us
  local copies, waits for them, and re-layouts: 3.65 us -> 0.63 us
    pallas_call x1, Pallas kernels: 50.9 us -> 44.3 us  [per_device(): pl.pallas_call(functools.partial(kernel, n_tm, n_chan), out_shape=jax.Sha...]
    unnamed x6 -> x1, local copies, waits for them, and re-layouts: 2.93 us -> 0.63 us
    pallas_call x1 -> x0, local copies, waits for them, and re-layouts: 0.72 us -> none  [per_device(): pl.pallas_call(functools.partial(kernel, n_tm, n_chan), out_shape=jax.Sha...]
where the time goes in v3:
time: 45.1 us; the launch traced here: 44.9 us
  Pallas kernels  44.3 us (98%)
  local copies, waits for them, and re-layouts  0.63 us (1%)
    pallas_call x1, Pallas kernels, per_device(): pl.pallas_call(functools.partial(kernel, n_tm, n_chan), out_shape=jax.Sha...  44.3 us

profile of v3, /device:TPU:1, one launch (start us, length us, event | category | flops | bytes accessed | tf_op | source)
XLA Modules:
  0.0 44.9 jit_solution(15562094090598119581)
XLA Ops:
  0.0 44.3 %shard_map.55 = f32[2,2,32,64]{3,2,1,0:T(8,128)S(1)} custom-call(s32[16]{0:T(128)} %m_hbm.1, s32[1,1024]{1,0:T(1,128)} %bitcast.3, bf16[64,32,512]{2,1,0:T(8,128)(2,1)} %vis_hbm.1, bf16[2,32,2,64,256]{4,3,2,1,0:T(8,128)(2,1)} %beam_hbm.1, f32[1024,1024]{1,0:T(8,128)} %cov_hbm.1), custom_call_target="tpu_custom_call" | custom-call | tf_op jit(solution)/shard_map/pallas_call | solution.py:238
  44.3 0.6 %copy.7 = f32[2,2,64,32]{2,3,1,0:T(8,128)} copy(f32[2,2,64,32]{2,3,1,0:T(8,128)S(1)} %bitcast.2) | data formatting | bytes 65536

commit v4 on v3

--- a/solution.py
+++ b/solution.py
@@ -31,8 +31,8 @@
 
 def kernel(
     n_tm, n_chan, m_hbm, flags_hbm, vis_hbm, beam_hbm, cov_hbm, out_ref,
-    m_ref, flags_ref, vis_v, beam_v, cov_v, pair_v, kron_v, part_v, got_v, give1, take1, give2, take2,
-    local_sem, psend, precv, send1, recv1, send2, recv2,
+    m_ref, flags_ref, vis_v, beam_v, cov_v, pair_v, kron_v, part_v, got_y, sum_y, got_y2, got_x, sum_x, got_x2, give1, take1, give2, take2,
+    local_sem, relay_sem, psend, precv, send1, recv1, send2, recv2,
 ):
     t_dev, f_dev, width = vis_v.shape
     half_w = width // 2
@@ -58,10 +58,28 @@
     flags_copy.start()
 
     barrier = pltpu.get_barrier_semaphore()
-    for i in range(1, n_tm):
-        pl.semaphore_signal(barrier, inc=1, device_id={"tm": lax.rem(my_tm + i, n_tm)}, device_id_type=MESH)
-    for i in range(1, n_chan):
-        pl.semaphore_signal(barrier, inc=1, device_id={"chan": lax.rem(my_chan + i, n_chan)}, device_id_type=MESH)
+    n_y = n_tm // 2
+    my_x, my_y = my_tm // n_y, lax.rem(my_tm, n_y)
+    n_w = 4
+    n_z = n_chan // n_w
+    my_z, my_w = my_chan // n_w, lax.rem(my_chan, n_w)
+
+    def tm_at(dx, dy):
+        return lax.rem(my_x + dx, 2) * n_y + lax.rem(my_y + dy, n_y)
+
+    def chan_at(dz, dw):
+        return lax.rem(my_z + dz, n_z) * n_w + lax.rem(my_w + dw, n_w)
+
+    near_tm = [(1, 0)] + [(0, dy) for dy in range(1, n_y)]
+    near_chan = [(dz, dw) for dz in (1, n_z - 1, 0) for dw in range(n_w) if (dz, dw) != (0, 0)]
+    for dx, dy in near_tm:
+        pl.semaphore_signal(barrier, inc=1, device_id={"tm": tm_at(dx, dy)}, device_id_type=MESH)
+    for dz, dw in near_chan:
+        pl.semaphore_signal(barrier, inc=1, device_id={"chan": chan_at(dz, dw)}, device_id_type=MESH)
+
+    def relay(i, dz):
+        for step in (dz, n_z - dz):
+            pl.semaphore_signal(relay_sem.at[i], inc=1, device_id={"chan": chan_at(step, 0)}, device_id_type=MESH)
 
     modes_copy.wait()
     row = lax.broadcasted_iota(jnp.int32, (n_m, t_dev), 0)
@@ -82,10 +100,22 @@
             kron_v[q, k * fh : (k + 1) * fh, :] = jnp.where(same, lanes[k : k + 1, :], 0.0).astype(jnp.bfloat16)
 
     scale = 1.0 / math.sqrt(n_time)
-    part_copies = ([], [])
+    far_first = [n_y // 2] + [dy for dy in range(1, n_y) if dy != n_y // 2]
+    sent = []
+
+    def push(src, dst, to):
+        i = len(sent)
+        copy = pltpu.make_async_remote_copy(
+            src_ref=src, dst_ref=dst, send_sem=psend.at[i], recv_sem=precv.at[i],
+            device_id={"tm": to}, device_id_type=MESH,
+        )
+        copy.start()
+        sent.append(copy)
+        return copy
+
     for h in range(2):
         vis_copies[h].wait()
-        if h == 1:
+        if h == 0:
             beam_copy = pltpu.make_async_copy(beam_hbm, beam_v, local_sem.at[2])
             cov_copy = pltpu.make_async_copy(cov_hbm, cov_v, local_sem.at[3])
             cov_copy.start()
@@ -98,16 +128,16 @@
         part_v[:, h, :, :half_w] = real.reshape(n_tm, m_dev * fh, half_w)
         part_v[:, h, :, half_w:] = imag.reshape(n_tm, m_dev * fh, half_w)
         if h == 0:
-            pl.semaphore_wait(barrier, n_tm - 1 + n_chan - 1)
-        for i in range(1, n_tm):
-            owner = lax.rem(my_tm + i, n_tm)
-            copy = pltpu.make_async_remote_copy(
-                src_ref=part_v.at[owner, h], dst_ref=got_v.at[i - 1, h],
-                send_sem=psend.at[i - 1, h], recv_sem=precv.at[i - 1, h],
-                device_id={"tm": owner}, device_id_type=MESH,
-            )
-            copy.start()
-            part_copies[h].append(copy)
+            pl.semaphore_wait(barrier, len(near_tm) + len(near_chan))
+            y_copies = [
+                {dy: push(part_v.at[tm_at(rel, dy), 0], got_y.at[dy - 1, rel], tm_at(0, dy)) for dy in far_first}
+                for rel in (1, 0)
+            ]
+            relay(0, 1)
+        else:
+            x_copies = {dy: push(part_v.at[tm_at(1, dy), 1], got_x.at[dy], tm_at(1, 0)) for dy in far_first}
+    pl.semaphore_wait(relay_sem.at[0], 2)
+    relay(1, 2)
 
     cov_copy.wait()
     step = 64
@@ -121,6 +151,19 @@
         pair_v[rows, :] = high
         pair_v[low_rows, :] = (block - high.astype(jnp.float32)).astype(jnp.bfloat16)
 
+    x2_copies, y2_copy = [], None
+    for dy in far_first:
+        x_copies[dy].wait_recv()
+        sum_x[dy - 1] = part_v[tm_at(0, dy), 1] + got_x[dy]
+        x2_copies.append(push(sum_x.at[dy - 1], got_x2.at[dy - 1], tm_at(0, dy)))
+        if y2_copy is None:
+            total = part_v[tm_at(1, 0), 0]
+            for step in far_first:
+                y_copies[0][step].wait_recv()
+                total = total + got_y[step - 1, 1]
+            sum_y[...] = total
+            y2_copy = push(sum_y, got_y2, tm_at(1, 0))
+            x_copies[0] = push(part_v.at[tm_at(1, 0), 1], got_x.at[0], tm_at(1, 0))
     beam_copy.wait()
     degrees = beam_v.shape[3]
     lanes = 2 * m_dev * f_dev
@@ -129,11 +172,19 @@
     coeffs = jnp.zeros((degrees, lanes), jnp.float32)
     blank = jnp.zeros((fh, half_w), jnp.float32)
     for h in range(2):
-        for copy in part_copies[h]:
-            copy.wait_recv()
         total = part_v[my_tm, h]
-        for i in range(n_tm - 1):
-            total = total + got_v[i, h]
+        if h == 0:
+            for dy in far_first:
+                y_copies[1][dy].wait_recv()
+                total = total + got_y[dy - 1, 0]
+            y2_copy.wait_recv()
+            total = total + got_y2[...]
+        else:
+            x_copies[0].wait_recv()
+            total = total + got_x[0]
+            for copy, dy in zip(x2_copies, far_first):
+                copy.wait_recv()
+                total = total + got_x2[dy - 1]
         mvis = total.astype(jnp.bfloat16).astype(jnp.float32)
         against_real, against_imag = [], []
         for m in range(m_dev):
@@ -159,6 +210,7 @@
                 coeffs = jnp.where(
                     lane_id == m * f_dev + h * fh + i, prod[i * degrees : (i + 1) * degrees, :], coeffs
                 )
+    pl.semaphore_wait(relay_sem.at[1], 2)
     pair = degrees // n_chan
     give1[...] = coeffs.reshape(n_chan, pair, lanes)
 
@@ -218,9 +270,8 @@
     tiles = swap_groups([filled[:, 128 * j : 128 * (j + 1)] for j in range(n_tiles)])
     give2[...] = jnp.concatenate(tiles, axis=0).reshape(n_chan, pair, lanes)
     exchange(give2, take2, send2, recv2)
-    for copies in part_copies:
-        for copy in copies:
-            copy.wait_send()
+    for copy in sent:
+        copy.wait_send()
     wait_all(give1, send1)
     wait_all(take2, recv2)
     back = take2[...].reshape(degrees, lanes)
@@ -233,6 +284,7 @@
     m_dev, _, _, degrees, half_w = beam.shape
     n_f = fg_cov.shape[0]
     lanes = 2 * m_dev * f_dev
+    piece = (m_dev * f_dev // 2, width)
     block = (n_chan, degrees // n_chan, lanes)
     hbm = pl.BlockSpec(memory_space=pltpu.HBM)
     filled = pl.pallas_call(
@@ -248,15 +300,21 @@
             pltpu.VMEM(fg_cov.shape, jnp.float32),
             pltpu.VMEM((2 * n_f, n_f), jnp.bfloat16),
             pltpu.VMEM((2, m_dev * n_tm * f_dev // 2, t_dev * f_dev // 2), jnp.bfloat16),
-            pltpu.VMEM((n_tm, 2, m_dev * f_dev // 2, width), jnp.float32),
-            pltpu.VMEM((n_tm - 1, 2, m_dev * f_dev // 2, width), jnp.float32),
+            pltpu.VMEM((n_tm, 2) + piece, jnp.float32),
+            pltpu.VMEM((n_tm // 2 - 1, 2) + piece, jnp.float32),
+            pltpu.VMEM(piece, jnp.float32),
+            pltpu.VMEM(piece, jnp.float32),
+            pltpu.VMEM((n_tm // 2,) + piece, jnp.float32),
+            pltpu.VMEM((n_tm // 2 - 1,) + piece, jnp.float32),
+            pltpu.VMEM((n_tm // 2 - 1,) + piece, jnp.float32),
             pltpu.VMEM(block, jnp.float32),
             pltpu.VMEM(block, jnp.float32),
             pltpu.VMEM(block, jnp.float32),
             pltpu.VMEM(block, jnp.float32),
             pltpu.SemaphoreType.DMA((6,)),
-            pltpu.SemaphoreType.DMA((n_tm - 1, 2)),
-            pltpu.SemaphoreType.DMA((n_tm - 1, 2)),
+            pltpu.SemaphoreType.REGULAR((2,)),
+            pltpu.SemaphoreType.DMA((14,)),
+            pltpu.SemaphoreType.DMA((14,)),
             pltpu.SemaphoreType.DMA((1,)),
             pltpu.SemaphoreType.DMA((1,)),
             pltpu.SemaphoreType.DMA((1,)),

time: 45.1 us -> 42.1 us (0.933)
  Pallas kernels: 44.3 us -> 41.4 us
    pallas_call x1, Pallas kernels: 44.3 us -> 41.4 us  [per_device(): pl.pallas_call(functools.partial(kernel, n_tm, n_chan), out_shape=jax.Sha...]
where the time goes in v4:
time: 42.1 us; the launch traced here: 42 us
  Pallas kernels  41.4 us (98%)
  local copies, waits for them, and re-layouts  0.63 us (1%)
    pallas_call x1, Pallas kernels, per_device(): pl.pallas_call(functools.partial(kernel, n_tm, n_chan), out_shape=jax.Sha...  41.4 us

profile of v4, /device:TPU:1, one launch (start us, length us, event | category | flops | bytes accessed | tf_op | source)
XLA Modules:
  0.0 42.0 jit_solution(4668327970099750102)
XLA Ops:
  0.0 41.4 %shard_map.55 = f32[2,2,32,64]{3,2,1,0:T(8,128)S(1)} custom-call(s32[16]{0:T(128)} %m_hbm.1, s32[1,1024]{1,0:T(1,128)} %bitcast.3, bf16[64,32,512]{2,1,0:T(8,128)(2,1)} %vis_hbm.1, bf16[2,32,2,64,256]{4,3,2,1,0:T(8,128)(2,1)} %beam_hbm.1, f32[1024,1024]{1,0:T(8,128)} %cov_hbm.1), custom_call_target="tpu_custom_call" | custom-call | tf_op jit(solution)/shard_map/pallas_call | solution.py:290
  41.4 0.6 %copy.7 = f32[2,2,64,32]{2,3,1,0:T(8,128)} copy(f32[2,2,64,32]{2,3,1,0:T(8,128)S(1)} %bitcast.2) | data formatting | bytes 65536

commit v5 on v4

--- a/solution.py
+++ b/solution.py
@@ -31,11 +31,12 @@
 
 def kernel(
     n_tm, n_chan, m_hbm, flags_hbm, vis_hbm, beam_hbm, cov_hbm, out_ref,
-    m_ref, flags_ref, vis_v, beam_v, cov_v, pair_v, kron_v, part_v, got_y, sum_y, got_y2, got_x, sum_x, got_x2, give1, take1, give2, take2,
-    local_sem, relay_sem, psend, precv, send1, recv1, send2, recv2,
+    m_ref, flags_ref, vis_v, beam_v, cov_v, pair_v, kron_v, part_v, got_y, sum_y, last_y, got_x, sum_x, last_x, give1, take1, give2, take2,
+    local_sem, vis_sem, relay_sem, psend, precv, send1, recv1, send2, recv2,
 ):
     t_dev, f_dev, width = vis_v.shape
     half_w = width // 2
+    quarter = half_w // 2
     n_m = m_ref.shape[0]
     m_dev = n_m // n_tm
     n_time = t_dev * n_tm
@@ -44,17 +45,17 @@
     my_tm = lax.axis_index("tm")
     my_chan = lax.axis_index("chan")
 
-    modes_copy = pltpu.make_async_copy(m_hbm, m_ref, local_sem.at[4])
+    modes_copy = pltpu.make_async_copy(m_hbm, m_ref, local_sem.at[0])
     modes_copy.start()
-    vis_copies = [
-        pltpu.make_async_copy(
-            vis_hbm.at[:, pl.ds(h * fh, fh), :], vis_v.at[:, pl.ds(h * fh, fh), :], local_sem.at[h]
-        )
-        for h in range(2)
-    ]
-    for copy in vis_copies:
-        copy.start()
-    flags_copy = pltpu.make_async_copy(flags_hbm, flags_ref, local_sem.at[5])
+    for h in range(2):
+        rows = pl.ds(h * fh, fh)
+        for j in range(2):
+            for at in (j * quarter, half_w + j * quarter):
+                pltpu.make_async_copy(
+                    vis_hbm.at[:, rows, pl.ds(at, quarter)], vis_v.at[:, rows, pl.ds(at, quarter)],
+                    vis_sem.at[2 * h + j],
+                ).start()
+    flags_copy = pltpu.make_async_copy(flags_hbm, flags_ref, local_sem.at[1])
     flags_copy.start()
 
     barrier = pltpu.get_barrier_semaphore()
@@ -97,45 +98,63 @@
     for q, table in enumerate((jnp.cos(angle), jnp.sin(angle))):
         lanes = jnp.dot(table.astype(jnp.bfloat16), spread, preferred_element_type=jnp.float32)
         for k in range(n_m):
-            kron_v[q, k * fh : (k + 1) * fh, :] = jnp.where(same, lanes[k : k + 1, :], 0.0).astype(jnp.bfloat16)
+            kron_v[(q * n_m + k) * fh : (q * n_m + k + 1) * fh, :] = jnp.where(same, lanes[k : k + 1, :], 0.0).astype(jnp.bfloat16)
 
     scale = 1.0 / math.sqrt(n_time)
     far_first = [n_y // 2] + [dy for dy in range(1, n_y) if dy != n_y // 2]
-    sent = []
-
-    def push(src, dst, to):
-        i = len(sent)
-        copy = pltpu.make_async_remote_copy(
-            src_ref=src, dst_ref=dst, send_sem=psend.at[i], recv_sem=precv.at[i],
+
+    def push(src, dst, arrival, to):
+        pltpu.make_async_remote_copy(
+            src_ref=src, dst_ref=dst, send_sem=psend.at[0], recv_sem=precv.at[arrival],
             device_id={"tm": to}, device_id_type=MESH,
-        )
-        copy.start()
-        sent.append(copy)
-        return copy
-
-    for h in range(2):
-        vis_copies[h].wait()
-        if h == 0:
+        ).start()
+
+    def arrived(dst, arrival):
+        pltpu.make_async_copy(dst, dst, precv.at[arrival]).wait()
+
+    def push_y(h, rel, dy):
+        to = (last_y.at[h, dy], 8 + h) if rel == 0 else (got_y.at[h, dy - 1], 6 + h)
+        push(part_v.at[tm_at(rel, dy), 2 * h], *to, tm_at(0, dy))
+
+    def push_x(h, dy):
+        to = (last_x.at[h, 0], 10 + h) if dy == 0 else (got_x.at[h, dy - 1], 3 * h + dy - 1)
+        push(part_v.at[tm_at(1, dy), 2 * h + 1], *to, tm_at(1, 0))
+
+    for chunk in range(4):
+        h, j = chunk // 2, chunk % 2
+        both = vis_v.at[:, pl.ds(h * fh, fh), pl.ds(0, half_w)]
+        pltpu.make_async_copy(both, both, vis_sem.at[chunk]).wait()
+        if chunk == 0:
             beam_copy = pltpu.make_async_copy(beam_hbm, beam_v, local_sem.at[2])
             cov_copy = pltpu.make_async_copy(cov_hbm, cov_v, local_sem.at[3])
             cov_copy.start()
             beam_copy.start()
-        data = vis_v[:, h * fh : (h + 1) * fh, :].reshape(t_dev * fh, width)
-        c = jnp.dot(kron_v[0], data, preferred_element_type=jnp.float32)
-        s = jnp.dot(kron_v[1], data, preferred_element_type=jnp.float32)
-        real = (c[:, :half_w] + s[:, half_w:]) * scale
-        imag = (c[:, half_w:] - s[:, :half_w]) * scale
-        part_v[:, h, :, :half_w] = real.reshape(n_tm, m_dev * fh, half_w)
-        part_v[:, h, :, half_w:] = imag.reshape(n_tm, m_dev * fh, half_w)
-        if h == 0:
+        data = jnp.concatenate(
+            [
+                vis_v[:, h * fh : (h + 1) * fh, at : at + quarter].reshape(t_dev * fh, quarter)
+                for at in (j * quarter, half_w + j * quarter)
+            ],
+            axis=1,
+        )
+        prod = jnp.dot(kron_v[...], data, preferred_element_type=jnp.float32)
+        c, s = prod[: n_m * fh, :], prod[n_m * fh :, :]
+        real = (c[:, :quarter] + s[:, quarter:]) * scale
+        imag = (c[:, quarter:] - s[:, :quarter]) * scale
+        part_v[:, chunk, :, :quarter] = real.reshape(n_tm, m_dev * fh, quarter)
+        part_v[:, chunk, :, quarter:] = imag.reshape(n_tm, m_dev * fh, quarter)
+        if chunk == 0:
             pl.semaphore_wait(barrier, len(near_tm) + len(near_chan))
-            y_copies = [
-                {dy: push(part_v.at[tm_at(rel, dy), 0], got_y.at[dy - 1, rel], tm_at(0, dy)) for dy in far_first}
-                for rel in (1, 0)
-            ]
+        if j == 0:
+            for dy in far_first:
+                push_y(h, 1, dy)
+        else:
+            for dy in far_first:
+                push_x(h, dy)
+        if chunk == 2:
+            for dy in far_first:
+                push_y(0, 0, dy)
+        if chunk == 0:
             relay(0, 1)
-        else:
-            x_copies = {dy: push(part_v.at[tm_at(1, dy), 1], got_x.at[dy], tm_at(1, 0)) for dy in far_first}
     pl.semaphore_wait(relay_sem.at[0], 2)
     relay(1, 2)
 
@@ -151,45 +170,47 @@
         pair_v[rows, :] = high
         pair_v[low_rows, :] = (block - high.astype(jnp.float32)).astype(jnp.bfloat16)
 
-    x2_copies, y2_copy = [], None
+    def forward_x(h, dy):
+        arrived(got_x.at[h, dy - 1], 3 * h + dy - 1)
+        sum_x[h, dy - 1] = part_v[tm_at(0, dy), 2 * h + 1] + got_x[h, dy - 1]
+        push(sum_x.at[h, dy - 1], last_x.at[h, dy], 10 + h, tm_at(0, dy))
+
+    def forward_y(h):
+        arrived(got_y.at[h], 6 + h)
+        total = part_v[tm_at(1, 0), 2 * h]
+        for dy in range(1, n_y):
+            total = total + got_y[h, dy - 1]
+        sum_y[h] = total
+        push(sum_y.at[h], last_y.at[h, 0], 8 + h, tm_at(1, 0))
+
+    forward_x(0, far_first[0])
+    forward_y(0)
+    for dy in far_first[1:]:
+        forward_x(0, dy)
+    forward_y(1)
+    push_x(0, 0)
     for dy in far_first:
-        x_copies[dy].wait_recv()
-        sum_x[dy - 1] = part_v[tm_at(0, dy), 1] + got_x[dy]
-        x2_copies.append(push(sum_x.at[dy - 1], got_x2.at[dy - 1], tm_at(0, dy)))
-        if y2_copy is None:
-            total = part_v[tm_at(1, 0), 0]
-            for step in far_first:
-                y_copies[0][step].wait_recv()
-                total = total + got_y[step - 1, 1]
-            sum_y[...] = total
-            y2_copy = push(sum_y, got_y2, tm_at(1, 0))
-            x_copies[0] = push(part_v.at[tm_at(1, 0), 1], got_x.at[0], tm_at(1, 0))
+        push_y(1, 0, dy)
+        forward_x(1, dy)
+    push_x(1, 0)
     beam_copy.wait()
     degrees = beam_v.shape[3]
     lanes = 2 * m_dev * f_dev
     lane = lax.broadcasted_iota(jnp.int32, (degrees, lanes), 1)
     lane_id = lane // (2 * f_dev) * f_dev + lane % f_dev
     coeffs = jnp.zeros((degrees, lanes), jnp.float32)
-    blank = jnp.zeros((fh, half_w), jnp.float32)
-    for h in range(2):
-        total = part_v[my_tm, h]
-        if h == 0:
-            for dy in far_first:
-                y_copies[1][dy].wait_recv()
-                total = total + got_y[dy - 1, 0]
-            y2_copy.wait_recv()
-            total = total + got_y2[...]
-        else:
-            x_copies[0].wait_recv()
-            total = total + got_x[0]
-            for copy, dy in zip(x2_copies, far_first):
-                copy.wait_recv()
-                total = total + got_x2[dy - 1]
+    blank = jnp.zeros((fh, quarter), jnp.float32)
+    for chunk in range(4):
+        h, j = chunk // 2, chunk % 2
+        total = part_v[my_tm, chunk]
+        last, arrival = ((last_y, 8), (last_x, 10))[j]
+        arrived(last.at[h], arrival + h)
+        for dy in range(n_y):
+            total = total + last[h, dy]
         mvis = total.astype(jnp.bfloat16).astype(jnp.float32)
         against_real, against_imag = [], []
         for m in range(m_dev):
-            block = mvis[m * fh : (m + 1) * fh, :]
-            re, im = block[:, :half_w], block[:, half_w:]
+            re, im = mvis[m * fh : (m + 1) * fh, :quarter], mvis[m * fh : (m + 1) * fh, quarter:]
             for first, second in ((re, -im), (im, re)):
                 against_real += [first, blank] if h == 0 else [blank, first]
                 against_imag += [second, blank] if h == 0 else [blank, second]
@@ -197,18 +218,18 @@
             [jnp.concatenate(against_real, axis=0).T, jnp.concatenate(against_imag, axis=0).T], axis=0
         ).astype(jnp.bfloat16)
         for m in range(m_dev):
-            rows = slice(h * fh, (h + 1) * fh)
             lhs = jnp.concatenate(
                 [
-                    beam_v[m, rows, 0].reshape(fh * degrees, half_w),
-                    beam_v[m, rows, 1].reshape(fh * degrees, half_w),
+                    beam_v[m, h * fh : (h + 1) * fh, p, :, j * quarter : (j + 1) * quarter].reshape(fh * degrees, quarter)
+                    for p in range(2)
                 ],
                 axis=1,
             )
             prod = jnp.dot(lhs, weights, preferred_element_type=jnp.float32)
             for i in range(fh):
+                here = prod[i * degrees : (i + 1) * degrees, :]
                 coeffs = jnp.where(
-                    lane_id == m * f_dev + h * fh + i, prod[i * degrees : (i + 1) * degrees, :], coeffs
+                    lane_id == m * f_dev + h * fh + i, here if j == 0 else coeffs + here, coeffs
                 )
     pl.semaphore_wait(relay_sem.at[1], 2)
     pair = degrees // n_chan
@@ -262,7 +283,7 @@
         return (signal, resid, direc, norm_next)
 
     signal, _, direc, norm_now = lax.fori_loop(
-        0, ITERS - 1, advance, (jnp.zeros_like(start), start, start, total_of(start * start))
+        0, ITERS - 1, advance, (jnp.zeros_like(start), start, start, total_of(start * start)), unroll=True
     )
     spread_out = apply_cov(direc)
     alpha = norm_now / (total_of(direc * (direc + good * spread_out)) + EPS)
@@ -270,8 +291,8 @@
     tiles = swap_groups([filled[:, 128 * j : 128 * (j + 1)] for j in range(n_tiles)])
     give2[...] = jnp.concatenate(tiles, axis=0).reshape(n_chan, pair, lanes)
     exchange(give2, take2, send2, recv2)
-    for copy in sent:
-        copy.wait_send()
+    all_sent = part_v.at[pl.ds(0, n_tm - 1)]
+    pltpu.make_async_copy(all_sent, all_sent, psend.at[0]).wait()
     wait_all(give1, send1)
     wait_all(take2, recv2)
     back = take2[...].reshape(degrees, lanes)
@@ -284,7 +305,7 @@
     m_dev, _, _, degrees, half_w = beam.shape
     n_f = fg_cov.shape[0]
     lanes = 2 * m_dev * f_dev
-    piece = (m_dev * f_dev // 2, width)
+    piece = (m_dev * f_dev // 2, width // 2)
     block = (n_chan, degrees // n_chan, lanes)
     hbm = pl.BlockSpec(memory_space=pltpu.HBM)
     filled = pl.pallas_call(
@@ -299,22 +320,23 @@
             pltpu.VMEM(beam.shape, beam.dtype),
             pltpu.VMEM(fg_cov.shape, jnp.float32),
             pltpu.VMEM((2 * n_f, n_f), jnp.bfloat16),
-            pltpu.VMEM((2, m_dev * n_tm * f_dev // 2, t_dev * f_dev // 2), jnp.bfloat16),
-            pltpu.VMEM((n_tm, 2) + piece, jnp.float32),
-            pltpu.VMEM((n_tm // 2 - 1, 2) + piece, jnp.float32),
-            pltpu.VMEM(piece, jnp.float32),
-            pltpu.VMEM(piece, jnp.float32),
-            pltpu.VMEM((n_tm // 2,) + piece, jnp.float32),
-            pltpu.VMEM((n_tm // 2 - 1,) + piece, jnp.float32),
-            pltpu.VMEM((n_tm // 2 - 1,) + piece, jnp.float32),
+            pltpu.VMEM((m_dev * n_tm * f_dev, t_dev * f_dev // 2), jnp.bfloat16),
+            pltpu.VMEM((n_tm, 4) + piece, jnp.float32),
+            pltpu.VMEM((2, n_tm // 2 - 1) + piece, jnp.float32),
+            pltpu.VMEM((2,) + piece, jnp.float32),
+            pltpu.VMEM((2, n_tm // 2) + piece, jnp.float32),
+            pltpu.VMEM((2, n_tm // 2 - 1) + piece, jnp.float32),
+            pltpu.VMEM((2, n_tm // 2 - 1) + piece, jnp.float32),
+            pltpu.VMEM((2, n_tm // 2) + piece, jnp.float32),
             pltpu.VMEM(block, jnp.float32),
             pltpu.VMEM(block, jnp.float32),
             pltpu.VMEM(block, jnp.float32),
             pltpu.VMEM(block, jnp.float32),
-            pltpu.SemaphoreType.DMA((6,)),
+            pltpu.SemaphoreType.DMA((4,)),
+            pltpu.SemaphoreType.DMA((4,)),
             pltpu.SemaphoreType.REGULAR((2,)),
-            pltpu.SemaphoreType.DMA((14,)),
-            pltpu.SemaphoreType.DMA((14,)),
+            pltpu.SemaphoreType.DMA((1,)),
+            pltpu.SemaphoreType.DMA((12,)),
             pltpu.SemaphoreType.DMA((1,)),
             pltpu.SemaphoreType.DMA((1,)),
             pltpu.SemaphoreType.DMA((1,)),

time: 42.1 us -> 41.4 us (0.983)
  Pallas kernels: 41.4 us -> 40.6 us
    pallas_call x1, Pallas kernels: 41.4 us -> 40.6 us  [per_device(): pl.pallas_call(functools.partial(kernel, n_tm, n_chan), out_shape=jax.Sha...]
where the time goes in v5:
time: 41.4 us; the launch traced here: 41.3 us
  Pallas kernels  40.6 us (98%)
  local copies, waits for them, and re-layouts  0.63 us (2%)
    pallas_call x1, Pallas kernels, per_device(): pl.pallas_call(functools.partial(kernel, n_tm, n_chan), out_shape=jax.Sha...  40.6 us

profile of v5, /device:TPU:1, one launch (start us, length us, event | category | flops | bytes accessed | tf_op | source)
XLA Modules:
  0.0 41.3 jit_solution(13695415909330073742)
XLA Ops:
  0.0 40.6 %shard_map.55 = f32[2,2,32,64]{3,2,1,0:T(8,128)S(1)} custom-call(s32[16]{0:T(128)} %m_hbm.1, s32[1,1024]{1,0:T(1,128)} %bitcast.3, bf16[64,32,512]{2,1,0:T(8,128)(2,1)} %vis_hbm.1, bf16[2,32,2,64,256]{4,3,2,1,0:T(8,128)(2,1)} %beam_hbm.1, f32[1024,1024]{1,0:T(8,128)} %cov_hbm.1), custom_call_target="tpu_custom_call" | custom-call | tf_op jit(solution)/shard_map/pallas_call | solution.py:311
  40.7 0.6 %copy.7 = f32[2,2,64,32]{2,3,1,0:T(8,128)} copy(f32[2,2,64,32]{2,3,1,0:T(8,128)S(1)} %bitcast.2) | data formatting | bytes 65536

commit v6 on v5

--- a/solution.py
+++ b/solution.py
@@ -47,17 +47,15 @@
 
     modes_copy = pltpu.make_async_copy(m_hbm, m_ref, local_sem.at[0])
     modes_copy.start()
-    for h in range(2):
+    def fetch(chunk):
+        h, j = chunk // 2, chunk % 2
         rows = pl.ds(h * fh, fh)
-        for j in range(2):
-            for at in (j * quarter, half_w + j * quarter):
-                pltpu.make_async_copy(
-                    vis_hbm.at[:, rows, pl.ds(at, quarter)], vis_v.at[:, rows, pl.ds(at, quarter)],
-                    vis_sem.at[2 * h + j],
-                ).start()
-    flags_copy = pltpu.make_async_copy(flags_hbm, flags_ref, local_sem.at[1])
-    flags_copy.start()
-
+        for at in (j * quarter, half_w + j * quarter):
+            pltpu.make_async_copy(
+                vis_hbm.at[:, rows, pl.ds(at, quarter)], vis_v.at[:, rows, pl.ds(at, quarter)], vis_sem.at[chunk]
+            ).start()
+
+    fetch(0)
     barrier = pltpu.get_barrier_semaphore()
     n_y = n_tm // 2
     my_x, my_y = my_tm // n_y, lax.rem(my_tm, n_y)
@@ -81,6 +79,11 @@
     def relay(i, dz):
         for step in (dz, n_z - dz):
             pl.semaphore_signal(relay_sem.at[i], inc=1, device_id={"chan": chan_at(step, 0)}, device_id_type=MESH)
+
+    for chunk in range(1, 4):
+        fetch(chunk)
+    flags_copy = pltpu.make_async_copy(flags_hbm, flags_ref, local_sem.at[1])
+    flags_copy.start()
 
     modes_copy.wait()
     row = lax.broadcasted_iota(jnp.int32, (n_m, t_dev), 0)
@@ -150,6 +153,8 @@
         else:
             for dy in far_first:
                 push_x(h, dy)
+            if h == 1:
+                push_x(0, 0)
         if chunk == 2:
             for dy in far_first:
                 push_y(0, 0, dy)
@@ -188,7 +193,6 @@
     for dy in far_first[1:]:
         forward_x(0, dy)
     forward_y(1)
-    push_x(0, 0)
     for dy in far_first:
         push_y(1, 0, dy)
         forward_x(1, dy)
@@ -200,8 +204,9 @@
     lane_id = lane // (2 * f_dev) * f_dev + lane % f_dev
     coeffs = jnp.zeros((degrees, lanes), jnp.float32)
     blank = jnp.zeros((fh, quarter), jnp.float32)
-    for chunk in range(4):
+    for chunk in (1, 0, 2, 3):
         h, j = chunk // 2, chunk % 2
+        first_of_half = chunk in (1, 2)
         total = part_v[my_tm, chunk]
         last, arrival = ((last_y, 8), (last_x, 10))[j]
         arrived(last.at[h], arrival + h)
@@ -229,7 +234,7 @@
             for i in range(fh):
                 here = prod[i * degrees : (i + 1) * degrees, :]
                 coeffs = jnp.where(
-                    lane_id == m * f_dev + h * fh + i, here if j == 0 else coeffs + here, coeffs
+                    lane_id == m * f_dev + h * fh + i, here if first_of_half else coeffs + here, coeffs
                 )
     pl.semaphore_wait(relay_sem.at[1], 2)
     pair = degrees // n_chan

time: 41.4 us -> 41.3 us (level)
  no operation moved by 1% of the time
where the time goes in v6:
time: 41.3 us; the launch traced here: 41.2 us
  Pallas kernels  40.6 us (98%)
  local copies, waits for them, and re-layouts  0.63 us (2%)
    pallas_call x1, Pallas kernels, per_device(): pl.pallas_call(functools.partial(kernel, n_tm, n_chan), out_shape=jax.Sha...  40.6 us

profile of v6, /device:TPU:1, one launch (start us, length us, event | category | flops | bytes accessed | tf_op | source)
XLA Modules:
  0.0 41.2 jit_solution(1940464154620630570)
XLA Ops:
  0.0 40.6 %shard_map.55 = f32[2,2,32,64]{3,2,1,0:T(8,128)S(1)} custom-call(s32[16]{0:T(128)} %m_hbm.1, s32[1,1024]{1,0:T(1,128)} %bitcast.3, bf16[64,32,512]{2,1,0:T(8,128)(2,1)} %vis_hbm.1, bf16[2,32,2,64,256]{4,3,2,1,0:T(8,128)(2,1)} %beam_hbm.1, f32[1024,1024]{1,0:T(8,128)} %cov_hbm.1), custom_call_target="tpu_custom_call" | custom-call | tf_op jit(solution)/shard_map/pallas_call | solution.py:316
  40.6 0.6 %copy.7 = f32[2,2,64,32]{2,3,1,0:T(8,128)} copy(f32[2,2,64,32]{2,3,1,0:T(8,128)S(1)} %bitcast.2) | data formatting | bytes 65536
